TPU v7x, 32 devices: a whole 2x2x4 slice. The times are simulated.
32 devices in a mesh: expert: 8 (over y, x, core), dp: 4 (over z).
Axes of the slice: x: 2, y: 2, z: 4, core: 2. Of those that a mesh axis runs over, the one named last changes fastest.
Arguments:
- tokens: bfloat16 [4096, 2048], P(('expert', 'dp')), may hold values from -6 to 6
- cotangent: bfloat16 [4096, 2048], P(('expert', 'dp')), may hold values from -6 to 6
- router_probs: float32 [4096, 6], P(('expert', 'dp')), may hold values from 0.1 to 0.6
- routes: int32 [4096, 6], P(('expert', 'dp')), may hold values from 0 to 15, all different within a row; in each aligned block of 128 rows (0 to 127, 128 to 255, ...) at most 60 rows name the same one
- partner: int32 [8], replicated, may hold values from 0 to 7, as said below
- gate_weight: bfloat16 [16, 2048, 768], P('expert'), may hold values from -0.125 to 0.125
- up_weight: bfloat16 [16, 2048, 768], P('expert'), may hold values from -0.125 to 0.125
- down_weight: bfloat16 [16, 768, 2048], P('expert'), may hold values from -0.21875 to 0.21875
Outputs:
- output: bfloat16 [4096, 2048], P(('expert', 'dp'))
- token_grad: bfloat16 [4096, 2048], P(('expert', 'dp'))
- expert_grads: bfloat16 [768, 16, 3, 2048], P('dp', 'expert')
Inputs may be any that keep to these rules, and one draw needn't show every extreme that they name: `routes`: each token names 6 different experts. Within the 128 rows of one device no expert is named by more than 60 rows, a bound that some block reaches of them. partner[j] is j or (j + 4) mod 8, and partner[partner[j]] = j.
All inputs are finite; a program needn't handle non-finite values.
Results may differ from a plain program's by a relative error of at most 0.0095.
Values may be sent and summed in bfloat16 or wider, within the bound.
A program may use at most 192 MiB of HBM per device.

v0:
```python
import jax
import jax.numpy as jnp
from jax import lax
from jax.sharding import PartitionSpec as P


def from_partner(value, axis, distance):
    mask = 2**distance
    pairs = [(source, source ^ mask) for source in range(lax.axis_size(axis))]
    return lax.ppermute(value, axis, pairs)


def forward_rows(rows_in, gate_part, up_part):
    gate_pre = jnp.einsum("necd,edf->necf", rows_in, gate_part, preferred_element_type=jnp.float32)
    up_proj = jnp.einsum("necd,edf->necf", rows_in, up_part, preferred_element_type=jnp.float32)
    sigmoid_gate = jax.nn.sigmoid(gate_pre)
    activated = gate_pre * sigmoid_gate
    hidden = (activated * up_proj).astype(jnp.bfloat16)
    return (gate_pre, up_proj, sigmoid_gate, activated, hidden)


def backward_rows(rows_cot, gate_pre, up_proj, sigmoid_gate, activated, down_part):
    grad_hidden = jnp.einsum(
        "necd,efd->necf", rows_cot, down_part, preferred_element_type=jnp.float32
    )
    grad_gate = (
        grad_hidden * up_proj * sigmoid_gate * (1.0 + gate_pre * (1.0 - sigmoid_gate))
    ).astype(jnp.bfloat16)
    grad_up = (grad_hidden * activated).astype(jnp.bfloat16)
    return (grad_gate, grad_up)


def input_grads(grad_gate, grad_up, gate_weight, up_weight):
    summed = jnp.einsum(
        "necf,edf->necd", grad_gate, gate_weight, preferred_element_type=jnp.float32
    )
    summed = summed + jnp.einsum(
        "necf,edf->necd", grad_up, up_weight, preferred_element_type=jnp.float32
    )
    return summed.astype(jnp.bfloat16)


def local(tokens, cotangent, router_probs, routes, partner, gate_weight, up_weight, down_weight):
    tok_dev = tokens.shape[0]
    model_width = tokens.shape[1]
    top_count = routes.shape[1]
    exp_dev = gate_weight.shape[0]
    hidden_units = gate_weight.shape[2]
    owners = lax.axis_size("expert")
    slot_total = exp_dev * owners
    capacity = max(2, 5 * tok_dev * top_count // (4 * slot_total))
    assigned = tok_dev * top_count
    flat_routes = routes.reshape(-1)
    blocks = flat_routes // exp_dev
    owner_ids = jnp.arange(owners, dtype=jnp.int32)
    target = jnp.sum(jnp.where(blocks[:, None] == owner_ids[None, :], partner[None, :], 0), axis=1)
    slot_key = target * exp_dev + flat_routes % exp_dev
    onehot = (slot_key[:, None] == jnp.arange(slot_total, dtype=jnp.int32)[None, :]).astype(
        jnp.int32
    )
    slot_rank = jnp.sum((jnp.cumsum(onehot, axis=0) - 1) * onehot, axis=1)
    slot_row = slot_key * capacity + slot_rank
    source = (
        jnp.full((slot_total * capacity,), assigned, jnp.int32)
        .at[slot_row]
        .set(jnp.arange(assigned, dtype=jnp.int32))
    )
    tok_index = source // top_count
    zero_row = jnp.zeros((1, model_width), jnp.bfloat16)
    padded_tokens = jnp.concatenate([tokens, zero_row], axis=0)
    padded_cot = jnp.concatenate([cotangent, zero_row], axis=0)
    padded_probs = jnp.concatenate([router_probs.reshape(-1), jnp.zeros((1,), jnp.float32)])
    send_tokens = padded_tokens[tok_index].reshape(owners, exp_dev, capacity, model_width)
    send_cot = (padded_probs[source][:, None] * padded_cot[tok_index].astype(jnp.float32)).astype(
        jnp.bfloat16
    )
    send_cot = send_cot.reshape(owners, exp_dev, capacity, model_width)
    recv_tokens, recv_cot = (
        lax.all_to_all(send_tokens, "expert", split_axis=0, concat_axis=0, tiled=True),
        lax.all_to_all(send_cot, "expert", split_axis=0, concat_axis=0, tiled=True),
    )
    gate_pre, up_proj, sigmoid_gate, activated, hidden = forward_rows(
        recv_tokens, gate_weight, up_weight
    )
    expert_out = jnp.einsum(
        "necf,efd->necd", hidden, down_weight, preferred_element_type=jnp.float32
    ).astype(jnp.bfloat16)
    grad_gate, grad_up = backward_rows(
        recv_cot, gate_pre, up_proj, sigmoid_gate, activated, down_weight
    )
    expert_dx = input_grads(grad_gate, grad_up, gate_weight, up_weight)
    back_out, back_dx = (
        lax.all_to_all(expert_out, "expert", split_axis=0, concat_axis=0, tiled=True),
        lax.all_to_all(expert_dx, "expert", split_axis=0, concat_axis=0, tiled=True),
    )
    picked_out = back_out.reshape(slot_total * capacity, model_width)[slot_row].reshape(
        tok_dev, top_count, model_width
    )
    picked_dx = back_dx.reshape(slot_total * capacity, model_width)[slot_row].reshape(
        tok_dev, top_count, model_width
    )
    output = jnp.sum(router_probs[:, :, None] * picked_out.astype(jnp.float32), axis=1).astype(
        jnp.bfloat16
    )
    token_grad = jnp.sum(picked_dx.astype(jnp.float32), axis=1).astype(jnp.bfloat16)
    quarter = hidden_units // lax.axis_size("dp")
    offset = lax.axis_index("dp") * quarter
    gate_part = lax.dynamic_slice_in_dim(gate_weight, offset, quarter, 2)
    up_part = lax.dynamic_slice_in_dim(up_weight, offset, quarter, 2)
    down_part = lax.dynamic_slice_in_dim(down_weight, offset, quarter, 1)
    rows_in = lax.all_gather(recv_tokens, "dp", axis=0, tiled=True)
    rows_cot = lax.all_gather(recv_cot, "dp", axis=0, tiled=True)
    shards = rows_in.shape[0] // owners
    part_gate, part_up, part_sigmoid, part_active, part_hidden = forward_rows(
        rows_in, gate_part, up_part
    )
    part_dgate, part_dup = backward_rows(
        rows_cot, part_gate, part_up, part_sigmoid, part_active, down_part
    )
    split_in = rows_in.reshape(shards, owners, exp_dev, capacity, model_width)
    split_cot = rows_cot.reshape(shards, owners, exp_dev, capacity, model_width)
    split_dgate = part_dgate.reshape(shards, owners, exp_dev, capacity, quarter)
    split_dup = part_dup.reshape(shards, owners, exp_dev, capacity, quarter)
    split_hidden = part_hidden.reshape(shards, owners, exp_dev, capacity, quarter)
    stacked = jnp.stack(
        [
            jnp.einsum(
                "snecf,snecd->sfed", split_dgate, split_in, preferred_element_type=jnp.float32
            ),
            jnp.einsum(
                "snecf,snecd->sfed", split_dup, split_in, preferred_element_type=jnp.float32
            ),
            jnp.einsum(
                "snecf,snecd->sfed", split_hidden, split_cot, preferred_element_type=jnp.float32
            ),
        ],
        axis=3,
    )
    rounded = lax.optimization_barrier(stacked.astype(jnp.bfloat16))
    summed = jnp.sum(rounded.astype(jnp.float32), axis=0)
    rounded_sum = summed.astype(jnp.bfloat16)
    row_here = lax.axis_index("expert")
    partner_here = jnp.sum(jnp.where(owner_ids == row_here, partner, 0))
    swap_bit = owners.bit_length() - 2
    swapped = from_partner(rounded_sum, "expert", swap_bit)
    expert_grads = jnp.where(partner_here == row_here, rounded_sum, swapped)
    return (output, token_grad, expert_grads)


def solution(mesh):
    placed = (
        P(("expert", "dp"), None),
        P(("expert", "dp"), None),
        P(("expert", "dp"), None),
        P(("expert", "dp"), None),
        P(),
        P("expert", None, None),
        P("expert", None, None),
        P("expert", None, None),
    )
    return jax.shard_map(
        local,
        mesh=mesh,
        in_specs=placed,
        out_specs=(
            P(("expert", "dp"), None),
            P(("expert", "dp"), None),
            P("dp", "expert", None, None),
        ),
        check_vma=False,
    )
```

profile of v0, /device:TPU:0, one launch (start us, length us, event | category | flops | bytes accessed | tf_op | source)
XLA Modules:
  0.0 953.1 jit_solution(2456945851649299749)
XLA Ops:
  7.2 0.8 copy.66
  8.0 0.1 reshape.202
  8.1 0.1 reshape.204
  8.3 0.1 reshape.203
  8.4 0.7 select_reduce_fusion
  9.2 1.7 reduce-window.6
  10.9 0.3 slice_reduce_fusion
  11.2 0.1 fusion.67
  11.4 3.4 scatter_custom_fusion
  14.8 1.1 concatenate.9
  15.9 6.0 gather_fusion
  21.9 4.9 reshape.206
  26.7 6.2 copy.70
  33.0 51.2 %all_to_all.20 = bf16[8,2,60,2048]{3,1,2,0:T(2,128)(2,1)S(1)} all-to-all(bf16[8,2,60,2048]{3,1,2,0:T(2,128)(2,1)S(1)} %copy.70), channel_id=1, replica_groups=mesh['expert'=8,'dp'=4] {'expert'}, dimensions={0} | all-to-all | bytes 7864320 | tf_op jit(solution)/shard_map/all_to_all | solution.py:79
  84.2 1.8 copy-done
  86.0 3.8 copy.71
  89.9 0.5 all-gather.5.cloned.1.call-start
  90.4 0.1 copy.65
  90.6 5.9 gather_fusion.3
  96.5 6.6 reshape.217
  103.1 0.1 reshape.208
  103.2 4.3 gather_fusion.2
  107.7 4.2 multiply_convert_fusion
  111.9 4.1 copy.76
  115.9 48.9 %all_to_all.21 = bf16[8,2,60,2048]{3,1,2,0:T(2,128)(2,1)S(1)} all-to-all(bf16[8,2,60,2048]{3,1,2,0:T(2,128)(2,1)S(1)} %copy.76), channel_id=1, replica_groups=mesh['expert'=8,'dp'=4] {'expert'}, dimensions={0} | all-to-all | bytes 7864320 | tf_op jit(solution)/shard_map/all_to_all | solution.py:80
  164.8 1.9 copy-done.2
  166.8 3.8 copy.77
  170.7 8.0 fusion.11
  178.8 4.0 fusion.15
  182.8 1.6 copy-done.12
  184.5 3.9 convert_bitcast_fusion
  188.4 5.9 copy.73
  194.3 4.7 all-to-all-start.1
  199.0 8.4 fusion.17
  207.4 1.8 copy-done.14
  209.2 5.7 fusion.9
  215.0 161.2 %all-gather.3.cloned.1.call-done = bf16[32,2,60,2048]{3,2,0,1:T(8,128)(2,1)} async-done(((bf16[8,2,60,2048]{3,2,0,1:T(8,128)(2,1)}), bf16[32,2,60,2048]{3,2,0,1:T(8,128)(2,1)}) %all-gather.3.cloned.1.call-update) | async-done | bytes 15728656 | tf_op jit(solution)/shard_map/all_gather | solution.py:111
  376.2 11.0 %fusion.52 = f32[2,192,32,60]{1,3,2,0:T(8,128)} fusion(bf16[32,2,60,2048]{3,2,0,1:T(8,128)(2,1)} %all-gather.3.cloned.1.call-done, bf16[2,2048,768]{2,1,0:T(8,128)(2,1)} %param.14, s32[]{:T(128)S(6)} %select_n.87), kind=kOutput, calls=%fused_computation.69 | convolution fusion | flops 3019898880 | bytes 21823492 | tf_op jit(solution)/shard_map/necd,edf->necf/dot_general | solution.py:15
  387.2 276.1 %all-gather.5.cloned.1.call-done = bf16[32,2,60,2048]{3,2,0,1:T(8,128)(2,1)} async-done(((bf16[8,2,60,2048]{3,2,0,1:T(8,128)(2,1)}), bf16[32,2,60,2048]{3,2,0,1:T(8,128)(2,1)}) %all-gather.5.cloned.1.call-update) | async-done | bytes 15728656 | tf_op jit(solution)/shard_map/all_gather | solution.py:112
  663.3 12.8 %fusion.62 = f32[2,192,32,60]{1,3,2,0:T(8,128)} fusion(bf16[32,2,60,2048]{3,2,0,1:T(8,128)(2,1)} %all-gather.5.cloned.1.call-done, bf16[2,768,2048]{2,1,0:T(8,128)(2,1)} %param.15, s32[]{:T(128)S(6)} %select_n.87), kind=kOutput, calls=%fused_computation.76 | convolution fusion | flops 3019898880 | bytes 21299204 | tf_op jit(solution)/shard_map/necd,efd->necf/dot_general | solution.py:23
  676.1 13.8 %fusion.33 = (bf16[32,2,60,192]{3,2,0,1:T(8,128)(2,1)}, bf16[32,2,60,192]{3,2,0,1:T(8,128)(2,1)S(1)}, bf16[32,2,60,192]{3,2,0,1:T(8,128)(2,1)}) fusion(f32[2,192,32,60]{1,3,2,0:T(8,128)} %fusion.52, f32[2,192,32,60]{1,3,2,0:T(8,128)} %fusion.62, bf16[32,2,60,2048]{3,2,0,1:T(8,128)(2,1)} %all-gather.3.cloned.1.call-done, bf16[2,2048,768]{2,1,0:T(8,128)(2,1)} %param.13, ...), kind=kOutput, calls=%fused_computation.44 | convolution fusion | flops 3030958080 | bytes 31686660 | tf_op jit(solution)/shard_map/necd,edf->necf/dot_general | solution.py:14
  689.9 9.9 %fusion.7 = bf16[4,192,2,1,2048]{4,1,2,0,3:T(8,128)(2,1)} fusion(bf16[4,8,2,60,2048]{4,3,1,0,2:T(8,128)(2,1)} %bitcast.187, bf16[4,8,2,60,192]{4,3,1,0,2:T(8,128)(2,1)} %bitcast.198), kind=kOutput, calls=%fused_computation.20 | convolution fusion | flops 3023044608 | bytes 23494656 | tf_op jit(solution)/shard_map/snecf,snecd->sfed/dot_general | solution.py:130
  699.8 9.9 %fusion.6 = bf16[4,192,2,1,2048]{4,1,2,0,3:T(8,128)(2,1)} fusion(bf16[4,8,2,60,2048]{4,3,1,0,2:T(8,128)(2,1)} %bitcast.188, bf16[4,8,2,60,192]{4,3,1,0,2:T(8,128)(2,1)} %bitcast.197), kind=kOutput, calls=%fused_computation.19 | convolution fusion | flops 3023044608 | bytes 23494656 | tf_op jit(solution)/shard_map/snecf,snecd->sfed/dot_general | solution.py:127
  709.7 9.4 fusion.8
  719.1 16.0 %pad_maximum_fusion = bf16[4,192,2,3,2048]{4,1,2,0,3:T(8,128)(2,1)} fusion(bf16[4,192,2,1,2048]{4,1,2,0,3:T(8,128)(2,1)} %fusion.8, bf16[4,192,2,1,2048]{4,1,2,0,3:T(8,128)(2,1)} %fusion.7, bf16[4,192,2,1,2048]{4,1,2,0,3:T(8,128)(2,1)} %fusion.6), kind=kLoop, calls=%fused_computation.6 | loop fusion | flops 18874368 | bytes 37748736 | tf_op jit(solution)/shard_map/stack | solution.py:125
  735.1 14.0 %reduce_sum.68 = bf16[192,2,3,2048]{3,0,1,2:T(8,128)(2,1)} reduce(bf16[4,192,2,3,2048]{4,1,2,0,3:T(8,128)(2,1)} %pad_maximum_fusion, bf16[]{:T(256)} %constant.35.clone.1), dimensions={0}, to_apply=%region_8.9 | reduce | flops 7077888 | bytes 23592962 | tf_op jit(solution)/shard_map/reduce_sum | solution.py:140
  749.1 1.5 collective-permute-start
  750.6 13.2 %fusion.27 = bf16[8,2,60,2048]{3,2,0,1:T(8,128)(2,1)} fusion(f32[2,8,60,2048]{3,2,1,0:T(8,128)} %fusion.9, bf16[2,2048,768]{2,1,0:T(8,128)(2,1)} %param.13, f32[2,8,60,768]{3,2,1,0:T(8,128)} %copy-done.14, f32[2,8,60,768]{3,2,1,0:T(8,128)S(1)} %copy-done.11, f32[2,8,60,768]{3,2,1,0:T(8,128)} %copy-done.12), kind=kOutput, calls=%fused_computation.35 | convolution fusion | flops 3031203840 | bytes 26935296 | tf_op jit(solution)/shard_map/necf,edf->necd/dot_general | solution.py:34
  763.8 8.1 copy.78
  771.9 4.9 all-to-all-start.3
  776.8 0.6 fusion.83
  778.0 5.9 copy.74
  783.9 4.9 reshape.207
  788.8 9.0 gather_fusion.1
  797.7 3.7 reshape.216
  801.5 93.8 %all-to-all-done.3 = bf16[8,2,60,2048]{3,1,2,0:T(2,128)(2,1)} async-done(((bf16[8,2,60,2048]{3,1,2,0:T(2,128)(2,1)}), bf16[8,2,60,2048]{3,1,2,0:T(2,128)(2,1)}, u32[]{:S(2)}, u32[]{:S(2)}) %all-to-all-start.3) | async-done | bytes 3932192 | tf_op jit(solution)/shard_map/all_to_all | solution.py:94
  895.3 5.9 copy.79
  901.2 4.9 reshape.209
  906.1 9.0 gather_fusion.4
  915.1 3.1 reshape.210
  918.2 5.7 reduce_sum.66
  923.9 7.5 multiply_reduce_fusion
  931.5 5.0 broadcast_select_fusion
  936.5 9.4 copy.90
  (64 shorter events, 0.4 us)
Async XLA Ops:
  7.2 369.0 %all-gather.3.cloned.1.call-start = ((), (), s32[]{:S(2)}) async-start(), calls=%async_computation.4 | async-start | bytes 20971520 | tf_op jit(solution)/shard_map/all_gather | solution.py:111
  11.4 3.4 copy-start.6
  84.2 1.9 copy-start
  86.0 4.4 copy-start.8
  86.0 4.5 copy-start.5
  89.9 573.4 %all-gather.5.cloned.1.call-start = ((), (), s32[]{:S(2)}) async-start(), calls=%async_computation.5 | async-start | bytes 20971520 | tf_op jit(solution)/shard_map/all_gather | solution.py:112
  90.5 12.5 %copy-start.3 = (f32[128,6]{1,0:T(8,128)}, f32[128,6]{1,0:T(8,128)S(1)}, u32[]{:S(2)}) copy-start(f32[128,6]{1,0:T(8,128)S(1)} %copy.65) | copy-start | bytes 9220
  164.8 1.9 copy-start.2
  170.6 8.1 slice-start.6
  170.6 8.1 copy-start.1
  170.7 8.1 slice-start.7
  170.7 13.8 %slice-start.4 = ((s8[6291456]{0:T(1024)(128)(4,1)}), s8[4194304]{0:T(1024)(128)(4,1)S(1)}, s32[]{:S(2)}) async-start(s8[6291456]{0:T(1024)(128)(4,1)} %bitcast.192), calls=%async_computation.10 | async-start | bytes 8388608
  178.8 4.1 copy-start.10
  178.8 5.7 slice-start.5
  182.8 1.6 copy-start.12
  194.3 14.9 %slice-start.2 = ((s8[6291456]{0:T(1024)(128)(4,1)}), s8[2097152]{0:T(1024)(128)(4,1)S(1)}, s32[]{:S(2)}) async-start(s8[6291456]{0:T(1024)(128)(4,1)} %bitcast.190), calls=%async_computation.8 | async-start | bytes 4194304
  194.3 577.6 %all-to-all-start.1 = ((bf16[8,2,60,2048]{3,1,2,0:T(2,128)(2,1)}), bf16[8,2,60,2048]{3,1,2,0:T(2,128)(2,1)}, u32[]{:S(2)}, u32[]{:S(2)}) async-start(bf16[8,2,60,2048]{3,1,2,0:T(2,128)(2,1)} %copy.73), calls=%async_computation.1 | async-start | bytes 7864320 | tf_op jit(solution)/shard_map/all_to_all | solution.py:93
  199.0 10.2 %slice-start.3 = ((s8[6291456]{0:T(1024)(128)(4,1)}), s8[4194304]{0:T(1024)(128)(4,1)S(1)}, s32[]{:S(2)}) async-start(s8[6291456]{0:T(1024)(128)(4,1)} %bitcast.190), calls=%async_computation.9 | async-start | bytes 8388608
  199.0 10.2 %copy-start.13 = (f32[2,8,60,768]{3,2,1,0:T(8,128)S(1)}, f32[2,8,60,768]{3,2,1,0:T(8,128)}, u32[]{:S(2)}) copy-start(f32[2,8,60,768]{3,2,1,0:T(8,128)} %copy-done.12) | copy-start | bytes 8847364
  207.4 1.8 copy-start.14
  735.1 15.4 %copy-start.11 = (f32[2,8,60,768]{3,2,1,0:T(8,128)S(1)}, f32[2,8,60,768]{3,2,1,0:T(8,128)}, u32[]{:S(2)}) copy-start(f32[2,8,60,768]{3,2,1,0:T(8,128)} %copy-done.10) | copy-start | bytes 8847364
  749.1 182.4 %collective-permute-start = (bf16[192,2,3,2048]{3,0,1,2:T(8,128)(2,1)}, bf16[192,2,3,2048]{3,0,1,2:T(8,128)(2,1)}, u32[]{:S(2)}, u32[]{:S(2)}) collective-permute-start(bf16[192,2,3,2048]{3,0,1,2:T(8,128)(2,1)} %reduce_sum.68), channel_id=1, source_target_pairs={{0,16},{4,20},{8,24},{12,28},{16,0},{20,4},{24,8},{28,12},{1,17},{... | collective-permute-start | bytes 14155784 | tf_op jit(solution)/shard_map/ppermute | solution.py:10
  771.9 4.9 copy-start.9
  771.9 6.1 copy-start.7
  771.9 123.3 %all-to-all-start.3 = ((bf16[8,2,60,2048]{3,1,2,0:T(2,128)(2,1)}), bf16[8,2,60,2048]{3,1,2,0:T(2,128)(2,1)}, u32[]{:S(2)}, u32[]{:S(2)}) async-start(bf16[8,2,60,2048]{3,1,2,0:T(2,128)(2,1)} %copy.78), calls=%async_computation.3 | async-start | bytes 7864320 | tf_op jit(solution)/shard_map/all_to_all | solution.py:94
  918.2 5.8 copy-start.4
  918.2 13.3 %slice-start = ((s8[4718592]{0:T(1024)(128)(4,1)}), s8[524288]{0:T(1024)(128)(4,1)S(1)}, s32[]{:S(2)}) async-start(s8[4718592]{0:T(1024)(128)(4,1)} %bitcast.184), calls=%async_computation.6 | async-start | bytes 1048576
  923.9 7.6 slice-start.1
Sparse Core Ops, SparseCore 0:
  90.0 286.1 all-gather.2
  378.3 284.9 all-gather.4
where the time goes:
time: 960 us; the launch traced here: 953 us
  waiting for transfers between devices  531 us (55%)
  local copies, waits for them, and re-layouts  129 us (13%)
  matrix products  110 us (11%)
  blocking collectives  100 us (10%)
  other arithmetic  55.7 us (6%)
  between operations  15.5 us (2%)
  starting transfers between devices  11.5 us (1%)
    all_gather x1, waiting for transfers between devices, local(): rows_cot = lax.all_gather(recv_cot, 'dp', axis=0, tiled=True)  276 us
    all_gather x1, waiting for transfers between devices, local(): rows_in = lax.all_gather(recv_tokens, 'dp', axis=0, tiled=True)  161 us
    all_to_all x1, waiting for transfers between devices, local(): lax.all_to_all(expert_dx, 'expert', split_axis=0, concat_axis=0, tiled=True)  93.8 us
    all_to_all x1, blocking collectives, local(): lax.all_to_all(send_tokens, 'expert', split_axis=0, concat_axis=0, tiled=...  51.2 us
    all_to_all x1, blocking collectives, local(): lax.all_to_all(send_cot, 'expert', split_axis=0, concat_axis=0, tiled=True)  48.9 us
    dot_general x2, matrix products, backward_rows(): jnp.einsum('necd,efd->necf', rows_cot, down_part, preferred_element_type=...  21.2 us
  transfers between devices with their start and end apart: 5, of which 3 were waited for; matrix products, arithmetic and copies ran while one was open for 26% of the time, Pallas kernels for 0%

commit v1 on v0

v1 whole, which is shorter than its diff:
```python
import jax
import jax.numpy as jnp
from jax import lax
from jax.sharding import PartitionSpec as P

BF = jnp.bfloat16
F32 = jnp.float32


def dot(a, b, dims):
    return lax.dot_general(a, b, (dims, ((), ())), preferred_element_type=F32)


def pick(onehot, block):
    rows = lax.dot_general(onehot, block, (((2,), (1,)), ((0,), (0,))), preferred_element_type=F32)
    return rows.reshape(-1, rows.shape[-1])


def select(routes, probs, expert, capacity):
    tok = routes.shape[2]
    hit = routes == expert
    mask = jnp.any(hit, axis=1)
    prob = jnp.sum(jnp.where(hit, probs, 0.0), axis=1)
    lower = (jnp.arange(tok)[:, None] <= jnp.arange(tok)[None, :]).astype(BF)
    rank = dot(mask.astype(BF), lower, ((1,), (0,))) - 1.0
    chosen = (rank[:, None, :] == jnp.arange(capacity, dtype=F32)[None, :, None]) & mask[:, None, :]
    row_prob = jnp.sum(jnp.where(chosen, prob[:, None, :], 0.0), axis=2)
    return chosen.astype(BF), row_prob.reshape(-1, 1)


def acts(x, c, gate_w, up_w, down_w):
    gate_pre = dot(x, gate_w, ((1,), (0,)))
    up_proj = dot(x, up_w, ((1,), (0,)))
    grad_hidden = dot(c, down_w, ((1,), (1,)))
    sig = jax.nn.sigmoid(gate_pre)
    active = gate_pre * sig
    hidden = (active * up_proj).astype(BF)
    dgate = (grad_hidden * up_proj * sig * (1.0 + gate_pre * (1.0 - sig))).astype(BF)
    dup = (grad_hidden * active).astype(BF)
    return dgate, dup, hidden


def local(tokens, cotangent, router_probs, routes, partner, gate_weight, up_weight, down_weight):
    tok, width = tokens.shape
    top = routes.shape[1]
    exp_dev = gate_weight.shape[0]
    units = gate_weight.shape[2]
    owners = lax.axis_size("expert")
    n_dp = lax.axis_size("dp")
    far = n_dp // 2
    capacity = max(2, 5 * tok * top // (4 * exp_dev * owners))
    capacity = -(-capacity // 16) * 16
    row_here = lax.axis_index("expert")
    z = lax.axis_index("dp")
    partner_here = jnp.sum(jnp.where(jnp.arange(owners) == row_here, partner, 0))
    half = units // far
    part_at = (z // 2) * half

    aux = jnp.concatenate([router_probs, routes.astype(F32)], axis=1).T
    aux_all = lax.all_gather(aux, ("expert", "dp"), axis=0).reshape(owners, n_dp, 2 * top, tok)

    def gathered(shift):
        moved = (tokens, cotangent)
        if shift:
            pairs = [((i + shift) % n_dp, i) for i in range(n_dp)]
            moved = tuple(lax.ppermute(v, "dp", pairs) for v in moved)
        x_all, c_all = (lax.all_gather(v, "expert", axis=0) for v in moved)
        own = lax.dynamic_index_in_dim(aux_all, lax.rem(z + shift, n_dp), 1, keepdims=False)
        return x_all, c_all, own[:, :top], own[:, top:]

    sets = [gathered(2 * h) for h in range(far)]

    outs, dxs, chosens = [], [], []
    pieces = []
    for s in range(exp_dev):
        expert = (partner_here * exp_dev + s).astype(F32)
        gate_w, up_w, down_w = gate_weight[s], up_weight[s], down_weight[s]
        lists = ([], [], [])
        rows = []
        for h, (x_all, c_all, probs, names) in enumerate(sets):
            chosen, row_prob = select(names, probs, expert, capacity)
            x = pick(chosen, x_all).astype(BF)
            c = (pick(chosen, c_all) * row_prob).astype(BF)
            if h == 0:
                dgate, dup, hidden = acts(x, c, gate_w, up_w, down_w)
                out = (dot(hidden, down_w, ((1,), (0,))) * row_prob).astype(BF)
                dx = (dot(dgate, gate_w, ((1,), (1,))) + dot(dup, up_w, ((1,), (1,)))).astype(BF)
                outs.append(out.reshape(owners, capacity, width))
                dxs.append(dx.reshape(owners, capacity, width))
                chosens.append(chosen)
                dgate, dup, hidden = (
                    lax.dynamic_slice_in_dim(v, part_at, half, 1) for v in (dgate, dup, hidden)
                )
            else:
                dgate, dup, hidden = acts(
                    x,
                    c,
                    lax.dynamic_slice_in_dim(gate_w, part_at, half, 1),
                    lax.dynamic_slice_in_dim(up_w, part_at, half, 1),
                    lax.dynamic_slice_in_dim(down_w, part_at, half, 0),
                )
            for kept, v in zip(lists, (dgate, dup, hidden)):
                kept.append(v)
            rows.append((x, x, c))
        for m in range(3):
            total = None
            for h in range(far):
                term = dot(lists[m][h], rows[h][m], ((0,), (0,)))
                total = term if total is None else total + term
            pieces.append(total.astype(BF))

    chosen = jnp.concatenate(chosens, axis=1)

    def back(values):
        stacked = jnp.concatenate(values, axis=1)
        summed = lax.dot_general(
            chosen, stacked, (((1,), (1,)), ((0,), (0,))), preferred_element_type=F32
        ).astype(BF)
        return lax.psum_scatter(summed, "expert", scatter_dimension=0, tiled=False)

    output = back(outs)
    token_grad = back(dxs)

    quarter = half // 2
    mine = lax.rem(z, 2)
    near = [(i, i ^ 1) for i in range(n_dp)]
    across = [(i, i ^ (owners // 2)) for i in range(owners)]
    finished = []
    for piece in pieces:
        kept = lax.dynamic_slice_in_dim(piece, mine * quarter, quarter, 0)
        sent = lax.dynamic_slice_in_dim(piece, (1 - mine) * quarter, quarter, 0)
        came = lax.ppermute(sent, "dp", near)
        summed = (kept.astype(F32) + came.astype(F32)).astype(BF)
        swapped = lax.ppermute(summed, "expert", across)
        finished.append(jnp.where(partner_here == row_here, summed, swapped))
    grads = jnp.stack(finished, axis=1).reshape(quarter, exp_dev, 3, width)
    return (output, token_grad, grads)


def solution(mesh):
    rows = P(("expert", "dp"), None)
    return jax.shard_map(
        local,
        mesh=mesh,
        in_specs=(rows, rows, rows, rows, P(), *[P("expert", None, None)] * 3),
        out_specs=(rows, rows, P("dp", "expert", None, None)),
        check_vma=False,
    )
```

time: 960 us -> 402 us (0.42)
  waiting for transfers between devices: 531 us -> 133 us
  local copies, waits for them, and re-layouts: 129 us -> 39.3 us
  other arithmetic: 55.7 us -> 15.3 us
  blocking collectives: 100 us -> 81.6 us
  matrix products: 110 us -> 97.2 us
    all_gather x2 -> x4, waiting for transfers between devices: 437 us -> 0.05 us  [gathered(): x_all, c_all = (lax.all_gather(v, 'expert', axis=0) for v in moved)]
    ppermute x1 -> x14, waiting for transfers between devices: 0.01 us -> 131 us  [the longest x6 78.3 us: local(): came = lax.ppermute(sent, 'dp', near)]
    all_to_all x2 -> x0, blocking collectives: 100 us -> none  [the longest x1 51.2 us: local(): lax.all_to_all(send_tokens, 'expert', split_axis=0, concat_axis=0, tiled=...]
    all_to_all x2 -> x0, waiting for transfers between devices: 93.8 us -> none  [the longest x1 93.8 us: local(): lax.all_to_all(expert_dx, 'expert', split_axis=0, concat_axis=0, tiled=True)]
    all_gather x0 -> x1, blocking collectives: none -> 81.6 us  [local(): lax.all_gather(aux, ('expert', 'dp'), axis=0)]
    gather x5 -> x0, local copies, waits for them, and re-layouts: 34.1 us -> none  [the longest x1 8.95 us: local(): back_out.reshape(slot_total * capacity, model_width)[slot_row]]
    convert_element_type x5 -> x0, local copies, waits for them, and re-layouts: 28.4 us -> none  [the longest x1 8.13 us: input_grads(): return summed.astype(jnp.bfloat16)]
    reduce_sum x6, other arithmetic: 28.7 us -> 3.3 us  [the longest x4 1.94 us: select(): row_prob = jnp.sum(jnp.where(chosen, prob[:, None, :], 0.0), axis=2)]
  transfers between devices with their start and end apart: 5 -> 20, of which waited for: 3 -> 10; matrix products, arithmetic and copies ran while one was open for 26% -> 36% of each run, Pallas kernels for 0% -> 0%
where the time goes in v1:
time: 402 us; the launch traced here: 397 us
  waiting for transfers between devices  133 us (33%)
  matrix products  97.2 us (24%)
  blocking collectives  81.6 us (20%)
  local copies, waits for them, and re-layouts  39.3 us (10%)
  between operations  16.4 us (4%)
  other arithmetic  15.3 us (4%)
  starting transfers between devices  14.4 us (4%)
    all_gather x1, blocking collectives, local(): lax.all_gather(aux, ('expert', 'dp'), axis=0)  81.6 us
    ppermute x6, waiting for transfers between devices, local(): came = lax.ppermute(sent, 'dp', near)  78.3 us
    dot_general x34, matrix products, dot(): return lax.dot_general(a, b, (dims, ((), ())), preferred_element_type=F32)  64.9 us
    ppermute x6, waiting for transfers between devices, local(): swapped = lax.ppermute(summed, 'expert', across)  29.6 us
    dot_general x8, matrix products, pick(): lax.dot_general(onehot, block, (((2,), (1,)), ((0,), (0,))), preferred_el...  26.2 us
    ppermute x2, waiting for transfers between devices, gathered(): moved = tuple((lax.ppermute(v, 'dp', pairs) for v in moved))  23.4 us
    unnamed x81, local copies, waits for them, and re-layouts  19.6 us
    slice x3, local copies, waits for them, and re-layouts, local(): gate_w, up_w, down_w = (gate_weight[s], up_weight[s], down_weight[s])  18.9 us
  transfers between devices with their start and end apart: 20, of which 10 were waited for; matrix products, arithmetic and copies ran while one was open for 36% of the time, Pallas kernels for 0%

profile of v1, /device:TPU:0, one launch (start us, length us, event | category | flops | bytes accessed | tf_op | source)
XLA Modules:
  0.0 396.8 jit_solution(17399917619522468830)
XLA Ops:
  8.7 4.1 %collective-permute-start.1 = (bf16[128,2048]{1,0:T(8,128)(2,1)}, bf16[128,2048]{1,0:T(8,128)(2,1)S(1)}, u32[]{:S(2)}, u32[]{:S(2)}) collective-permute-start(bf16[128,2048]{1,0:T(8,128)(2,1)} %param.8), channel_id=1, source_target_pairs={{2,0},{3,1},{0,2},{1,3},{6,4},{7,5},{4,6},{5,7},{10,8},{11,9},{8,1... | collective-permute-start | bytes 1572872 | tf_op jit(solution)/shard_map/ppermute | solution.py:66
  12.8 23.4 %collective-permute-done.1 = bf16[128,2048]{1,0:T(8,128)(2,1)S(1)} collective-permute-done((bf16[128,2048]{1,0:T(8,128)(2,1)}, bf16[128,2048]{1,0:T(8,128)(2,1)S(1)}, u32[]{:S(2)}, u32[]{:S(2)}) %collective-permute-start.1) | collective-permute-done | bytes 524320 | tf_op jit(solution)/shard_map/ppermute | solution.py:66
  37.2 1.3 fusion.114
  41.2 81.6 %all-gather.5 = f32[32,12,128]{2,1,0:T(8,128)S(1)} all-gather(f32[1,12,128]{2,1,0:T(8,128)S(1)} %maximum_bitcast_fusion), channel_id=2, replica_groups=mesh['expert'=8,'dp'=4] {'expert','dp'}, dimensions={0}, use_global_device_ids=true | all-gather | bytes 202752 | tf_op jit(solution)/shard_map/all_gather | solution.py:60
  126.5 5.8 %fusion.145 = (bf16[1,2048,768]{2,1,0:T(8,128)(2,1)}, bf16[1,2048,768]{2,1,0:T(8,128)(2,1)}) fusion(bf16[2,2048,768]{2,1,0:T(8,128)(2,1)} %param.13), kind=kLoop, calls=%fused_computation.207 | loop fusion | bytes 12582912 | tf_op jit(solution)/shard_map/slice | solution.py:77
  133.5 6.0 %fusion.143 = (bf16[1,2048,768]{2,1,0:T(8,128)(2,1)}, bf16[1,2048,768]{2,1,0:T(8,128)(2,1)}) fusion(bf16[2,2048,768]{2,1,0:T(8,128)(2,1)} %param.14), kind=kLoop, calls=%fused_computation.205 | loop fusion | bytes 12582912 | tf_op jit(solution)/shard_map/slice | solution.py:77
  139.5 4.9 %convolution_convert_fusion.3 = bf16[8,64,2048]{2,1,0:T(8,128)(2,1)} fusion(bf16[8,128,2048]{2,1,0:T(8,128)(2,1)} %bitcast.164, f32[8,128]{1,0:T(8,128)S(1)} %convolution_add_fusion.3, pred[8,128]{1,0:T(8,128)(4,1)S(1)} %get-tuple-element.16), kind=kOutput, calls=%fused_computation.57 | convolution fusion | flops 269615104 | bytes 6296576 | tf_op jit(solution)/shard_map/dot_general | solution.py:15
  144.3 1.2 convolution_convert_fusion.2
  145.6 5.6 %multiply_convert_fusion.3 = (bf16[8,64,2048]{2,1,0:T(8,128)(2,1)S(1)}, f32[8,64,2048]{2,1,0:T(8,128)}) fusion(f32[8,64]{1,0:T(8,128)S(1)} %select_reduce_fusion.3, bf16[8,128,2048]{2,1,0:T(8,128)(2,1)} %bitcast.166, f32[8,128]{1,0:T(8,128)S(1)} %convolution_add_fusion.3, pred[8,128]{1,0:T(8,128)(4,1)S(1)} %get-tuple-element.16), kind=kOutput, calls=%fused_computation.21 | convolution fusion | flops 270663680 | bytes 10492928 | tf_op jit(solution)/shard_map/dot_general | solution.py:15
  151.2 4.3 %fusion.34 = f32[512,768]{1,0:T(8,128)S(1)} fusion(bf16[512,2048]{1,0:T(8,128)(2,1)S(1)} %bitcast.159, bf16[2,2048,768]{2,1,0:T(8,128)(2,1)} %param.14), kind=kOutput, calls=%fused_computation.42 | convolution fusion | flops 1610612736 | bytes 6815744 | tf_op jit(solution)/shard_map/dot_general | solution.py:11
  155.6 1.9 fusion.29
  157.5 3.5 multiply_convert_fusion.9
  160.9 1.8 multiply_convert_fusion.5
  163.2 3.4 multiply_convert_fusion.2
  166.5 1.8 fusion.23
  168.3 1.8 fusion.18
  170.2 3.4 multiply_convert_fusion.7
  173.6 1.8 multiply_convert_fusion.4
  175.4 2.9 fusion.15
  178.4 7.2 %fusion.144 = (bf16[1,768,2048]{2,1,0:T(8,128)(2,1)}, bf16[1,768,2048]{2,1,0:T(8,128)(2,1)}) fusion(bf16[2,768,2048]{2,1,0:T(8,128)(2,1)} %param.15), kind=kLoop, calls=%fused_computation.206 | loop fusion | bytes 12582912 | tf_op jit(solution)/shard_map/slice | solution.py:77
  185.6 4.2 %fusion.21 = f32[512,2048]{1,0:T(8,128)S(1)} fusion(bf16[512,768]{1,0:T(8,128)(2,1)S(1)} %copy-done.28, bf16[2,2048,768]{2,1,0:T(8,128)(2,1)} %param.14), kind=kOutput, calls=%fused_computation.29 | convolution fusion | flops 1610612736 | bytes 8126464 | tf_op jit(solution)/shard_map/dot_general | solution.py:11
  189.8 3.9 fusion.32
  193.7 1.8 add_convert_fusion
  195.6 1.8 add_convert_fusion.1
  197.4 3.1 fusion.12
  200.5 4.5 %fusion.88 = f32[384,2048]{1,0:T(8,128)} fusion(bf16[512,2048]{1,0:T(8,128)(2,1)} %bitcast.158, bf16[512,768]{1,0:T(8,128)(2,1)} %get-tuple-element.25, s32[]{:T(128)S(6)} %select_n.108), kind=kOutput, calls=%fused_computation.139 | convolution fusion | flops 805306368 | bytes 5636100 | tf_op jit(solution)/shard_map/dot_general | solution.py:11
  205.0 2.7 fusion.84
  207.7 2.7 fusion.80
  210.4 2.7 fusion.78
  213.5 2.7 fusion.82
  217.4 2.7 fusion.76
  220.1 3.5 convolution_convert_fusion
  223.6 2.5 convolution_convert_fusion.1
  226.2 3.4 multiply_convert_fusion.1
  229.6 1.8 multiply_convert_fusion
  231.5 1.3 fusion.44
  233.3 1.3 fusion.46
  235.4 1.3 fusion.50
  237.0 1.3 fusion.52
  238.9 1.9 copy-done.13
  243.1 1.1 add_convert_fusion.2
  244.4 2.0 collective-permute-start.6
  246.4 1.3 fusion.54
  247.7 1.2 add_convert_fusion.7
  251.5 1.3 fusion.48
  252.8 1.2 add_convert_fusion.4
  254.7 1.1 add_convert_fusion.3
  256.3 1.9 collective-permute-start.4
  258.6 6.2 %collective-permute-done.12 = bf16[192,2048]{1,0:T(8,128)(2,1)S(1)} collective-permute-done((bf16[192,2048]{1,0:T(8,128)(2,1)S(1)}, bf16[192,2048]{1,0:T(8,128)(2,1)S(1)}, u32[]{:S(2)}, u32[]{:S(2)}) %collective-permute-start.12) | collective-permute-done | bytes 786464 | tf_op jit(solution)/shard_map/ppermute | solution.py:132
  265.1 16.6 %collective-permute-done.6 = bf16[192,2048]{1,0:T(8,128)(2,1)S(1)} collective-permute-done((bf16[192,2048]{1,0:T(8,128)(2,1)S(1)}, bf16[192,2048]{1,0:T(8,128)(2,1)S(1)}, u32[]{:S(2)}, u32[]{:S(2)}) %collective-permute-start.6) | collective-permute-done | bytes 786464 | tf_op jit(solution)/shard_map/ppermute | solution.py:132
  282.6 15.8 %collective-permute-done.2 = bf16[192,2048]{1,0:T(8,128)(2,1)S(1)} collective-permute-done((bf16[192,2048]{1,0:T(8,128)(2,1)S(1)}, bf16[192,2048]{1,0:T(8,128)(2,1)S(1)}, u32[]{:S(2)}, u32[]{:S(2)}) %collective-permute-start.2) | collective-permute-done | bytes 786464 | tf_op jit(solution)/shard_map/ppermute | solution.py:132
  299.5 15.8 %collective-permute-done.4 = bf16[192,2048]{1,0:T(8,128)(2,1)S(1)} collective-permute-done((bf16[192,2048]{1,0:T(8,128)(2,1)S(1)}, bf16[192,2048]{1,0:T(8,128)(2,1)S(1)}, u32[]{:S(2)}, u32[]{:S(2)}) %collective-permute-start.4) | collective-permute-done | bytes 786464 | tf_op jit(solution)/shard_map/ppermute | solution.py:132
  316.4 15.8 %collective-permute-done.8 = bf16[192,2048]{1,0:T(8,128)(2,1)S(1)} collective-permute-done((bf16[192,2048]{1,0:T(8,128)(2,1)S(1)}, bf16[192,2048]{1,0:T(8,128)(2,1)S(1)}, u32[]{:S(2)}, u32[]{:S(2)}) %collective-permute-start.8) | collective-permute-done | bytes 786464 | tf_op jit(solution)/shard_map/ppermute | solution.py:132
  333.2 8.0 %collective-permute-done.10 = bf16[192,2048]{1,0:T(8,128)(2,1)S(1)} collective-permute-done((bf16[192,2048]{1,0:T(8,128)(2,1)S(1)}, bf16[192,2048]{1,0:T(8,128)(2,1)S(1)}, u32[]{:S(2)}, u32[]{:S(2)}) %collective-permute-start.10) | collective-permute-done | bytes 786464 | tf_op jit(solution)/shard_map/ppermute | solution.py:132
  343.6 1.2 bitcast_dynamic-update-slice_fusion.5
  344.8 7.4 %collective-permute-done.5 = bf16[192,2048]{1,0:T(8,128)(2,1)S(1)} collective-permute-done((bf16[192,2048]{1,0:T(8,128)(2,1)S(1)}, bf16[192,2048]{1,0:T(8,128)(2,1)S(1)}, u32[]{:S(2)}, u32[]{:S(2)}) %collective-permute-start.5) | collective-permute-done | bytes 786464 | tf_op jit(solution)/shard_map/ppermute | solution.py:134
  352.2 1.2 bitcast_dynamic-update-slice_fusion.4
  353.4 1.2 bitcast_dynamic-update-slice_fusion.3
  354.5 14.5 %collective-permute-done.9 = bf16[192,2048]{1,0:T(8,128)(2,1)S(1)} collective-permute-done((bf16[192,2048]{1,0:T(8,128)(2,1)S(1)}, bf16[192,2048]{1,0:T(8,128)(2,1)S(1)}, u32[]{:S(2)}, u32[]{:S(2)}) %collective-permute-start.9) | collective-permute-done | bytes 786464 | tf_op jit(solution)/shard_map/ppermute | solution.py:134
  369.0 1.2 bitcast_dynamic-update-slice_fusion.2
  370.2 7.7 %collective-permute-done.11 = bf16[192,2048]{1,0:T(8,128)(2,1)S(1)} collective-permute-done((bf16[192,2048]{1,0:T(8,128)(2,1)S(1)}, bf16[192,2048]{1,0:T(8,128)(2,1)S(1)}, u32[]{:S(2)}, u32[]{:S(2)}) %collective-permute-start.11) | collective-permute-done | bytes 786464 | tf_op jit(solution)/shard_map/ppermute | solution.py:134
  377.9 1.2 bitcast_dynamic-update-slice_fusion.1
  379.1 1.2 bitcast_dynamic-update-slice_fusion
  380.3 9.4 %copy.28 = bf16[192,2,3,2048]{3,1,2,0:T(2,128)(2,1)} copy(bf16[192,2,3,2048]{3,0,2,1:T(8,128)(2,1)} %bitcast.45) | data formatting | bytes 9437184
  (156 shorter events, 26.5 us)
Async XLA Ops:
  7.2 132.3 %all-gather.11.cloned.1.call-start = ((), (), s32[]{:S(2)}) async-start(), calls=%async_computation.4 | async-start | bytes 4718592 | tf_op jit(solution)/shard_map/all_gather | solution.py:67
  7.9 137.6 %all-gather.13.cloned.1.call-start = ((), (), s32[]{:S(2)}) async-start(), calls=%async_computation.5 | async-start | bytes 4718592 | tf_op jit(solution)/shard_map/all_gather | solution.py:67
  8.6 211.4 %all-gather.17.cloned.1.call-start = ((), (), s32[]{:S(2)}) async-start(), calls=%async_computation.7 | async-start | bytes 4718592 | tf_op jit(solution)/shard_map/all_gather | solution.py:67
  8.7 27.5 %collective-permute-start.1 = (bf16[128,2048]{1,0:T(8,128)(2,1)}, bf16[128,2048]{1,0:T(8,128)(2,1)S(1)}, u32[]{:S(2)}, u32[]{:S(2)}) collective-permute-start(bf16[128,2048]{1,0:T(8,128)(2,1)} %param.8), channel_id=1, source_target_pairs={{2,0},{3,1},{0,2},{1,3},{6,4},{7,5},{4,6},{5,7},{10,8},{11,9},{8,1... | collective-permute-start | bytes 1572872 | tf_op jit(solution)/shard_map/ppermute | solution.py:66
  36.2 0.8 copy-start.21
  37.0 189.1 %all-gather.15.cloned.1.call-start = ((), (), s32[]{:S(2)}) async-start(), calls=%async_computation.6 | async-start | bytes 4718592 | tf_op jit(solution)/shard_map/all_gather | solution.py:67
  37.1 95.2 %collective-permute-start = (bf16[128,2048]{1,0:T(8,128)(2,1)}, bf16[128,2048]{1,0:T(8,128)(2,1)S(1)}, u32[]{:S(2)}, u32[]{:S(2)}) collective-permute-start(bf16[128,2048]{1,0:T(8,128)(2,1)} %param.9), channel_id=1, source_target_pairs={{2,0},{3,1},{0,2},{1,3},{6,4},{7,5},{4,6},{5,7},{10,8},{11,9},{8,1... | collective-permute-start | bytes 1572872 | tf_op jit(solution)/shard_map/ppermute | solution.py:66
  132.3 0.8 copy-start.22
  133.2 256.5 %reduce-scatter.3.cloned.1.call-start = ((), (), s32[]{:S(2)}) async-start(), calls=%async_computation.2 | async-start | bytes 4718592 | tf_op jit(solution)/shard_map/reduce_scatter | solution.py:119
  139.5 4.9 %copy-start.3 = (bf16[1024,2048]{1,0:T(8,128)(2,1)S(1)}, bf16[1024,2048]{1,0:T(8,128)(2,1)}, u32[]{:S(2)}) copy-start(bf16[1024,2048]{1,0:T(8,128)(2,1)} %all-gather.11.cloned.1.call-done) | copy-start | bytes 12582916
  145.5 5.6 %copy-start = (bf16[8,64,2048]{2,1,0:T(8,128)(2,1)S(1)}, bf16[8,64,2048]{2,1,0:T(8,128)(2,1)}, u32[]{:S(2)}) copy-start(bf16[8,64,2048]{2,1,0:T(8,128)(2,1)} %convolution_convert_fusion.3) | copy-start | bytes 6291460
  145.5 10.0 %slice-start = ((s8[6291456]{0:T(1024)(128)(4,1)}), s8[4194304]{0:T(1024)(128)(4,1)S(1)}, s32[]{:S(2)}) async-start(s8[6291456]{0:T(1024)(128)(4,1)} %bitcast.178), calls=%async_computation.8 | async-start | bytes 8388608
  151.2 4.4 %slice-start.1 = ((s8[6291456]{0:T(1024)(128)(4,1)}), s8[2097152]{0:T(1024)(128)(4,1)S(1)}, s32[]{:S(2)}) async-start(s8[6291456]{0:T(1024)(128)(4,1)} %bitcast.178), calls=%async_computation.9 | async-start | bytes 4194304
  151.2 6.3 %slice-start.4 = ((s8[6291456]{0:T(1024)(128)(4,1)}), s8[4194304]{0:T(1024)(128)(4,1)S(1)}, s32[]{:S(2)}) async-start(s8[6291456]{0:T(1024)(128)(4,1)} %bitcast.182), calls=%async_computation.12 | async-start | bytes 8388608
  155.5 2.0 slice-start.5
  160.9 2.2 copy-start.4
  160.9 5.6 %slice-start.2 = ((s8[6291456]{0:T(1024)(128)(4,1)}), s8[4194304]{0:T(1024)(128)(4,1)S(1)}, s32[]{:S(2)}) async-start(s8[6291456]{0:T(1024)(128)(4,1)} %bitcast.180), calls=%async_computation.10 | async-start | bytes 8388608
  163.2 3.4 slice-start.3
  173.6 1.8 copy-start.25
  178.3 211.3 %reduce-scatter.5.cloned.1.call-start = ((), (), s32[]{:S(2)}) async-start(), calls=%async_computation.3 | async-start | bytes 4718592 | tf_op jit(solution)/shard_map/reduce_scatter | solution.py:119
  178.4 7.2 %copy-start.28 = (bf16[512,768]{1,0:T(8,128)(2,1)S(1)}, bf16[512,768]{1,0:T(8,128)(2,1)}, u32[]{:S(2)}) copy-start(bf16[512,768]{1,0:T(8,128)(2,1)} %get-tuple-element.29) | copy-start | bytes 2359300
  185.6 4.2 %copy-start.23 = (bf16[512,768]{1,0:T(8,128)(2,1)S(1)}, bf16[512,768]{1,0:T(8,128)(2,1)}, u32[]{:S(2)}) copy-start(bf16[512,768]{1,0:T(8,128)(2,1)} %get-tuple-element.26) | copy-start | bytes 2359300
  185.6 8.1 %slice-start.6 = ((s8[6291456]{0:T(1024)(128)(4,1)}), s8[4194304]{0:T(1024)(128)(4,1)S(1)}, s32[]{:S(2)}) async-start(s8[6291456]{0:T(1024)(128)(4,1)} %bitcast.184), calls=%async_computation.14 | async-start | bytes 8388608
  189.8 3.9 slice-start.7
  189.8 3.9 copy-start.30
  193.7 1.8 copy-start.27
  200.5 4.5 %copy-start.1 = (bf16[8,64,2048]{2,1,0:T(8,128)(2,1)S(1)}, bf16[8,64,2048]{2,1,0:T(8,128)(2,1)}, u32[]{:S(2)}) copy-start(bf16[8,64,2048]{2,1,0:T(8,128)(2,1)} %convolution_convert_fusion.3) | copy-start | bytes 6291460
  200.5 4.5 %copy-start.24 = (bf16[512,768]{1,0:T(8,128)(2,1)S(1)}, bf16[512,768]{1,0:T(8,128)(2,1)}, u32[]{:S(2)}) copy-start(bf16[512,768]{1,0:T(8,128)(2,1)} %get-tuple-element.26) | copy-start | bytes 2359300
  205.0 2.7 copy-start.31
  207.7 2.7 copy-start.29
  210.4 2.8 copy-start.6
  213.5 2.7 copy-start.7
  216.2 1.1 copy-start.26
  220.1 3.5 copy-start.2
  226.2 3.5 copy-start.5
  229.6 1.9 copy-start.16
  231.4 1.9 copy-start.18
  232.8 1.8 copy-start.10
  232.8 2.6 copy-start.15
  234.6 2.4 copy-start.17
  238.6 2.2 copy-start.13
  240.8 2.2 copy-start.14
  243.1 3.3 copy-start.20
  244.3 3.4 copy-start.9
  244.3 20.5 %collective-permute-start.12 = (bf16[192,2048]{1,0:T(8,128)(2,1)S(1)}, bf16[192,2048]{1,0:T(8,128)(2,1)S(1)}, u32[]{:S(2)}, u32[]{:S(2)}) collective-permute-start(bf16[192,2048]{1,0:T(8,128)(2,1)S(1)} %constant_dynamic-slice_fusion), channel_id=1, source_target_pairs={{0,1},{1,0},{2,3},{3,2},{4,5},{5,4},{6,7},{7,6},{8,9},{9,8},{10,11... | collective-permute-start | bytes 2359304 | tf_op jit(solution)/shard_map/ppermute | solution.py:132
  244.4 37.3 %collective-permute-start.6 = (bf16[192,2048]{1,0:T(8,128)(2,1)S(1)}, bf16[192,2048]{1,0:T(8,128)(2,1)S(1)}, u32[]{:S(2)}, u32[]{:S(2)}) collective-permute-start(bf16[192,2048]{1,0:T(8,128)(2,1)S(1)} %constant_dynamic-slice_fusion.3), channel_id=1, source_target_pairs={{0,1},{1,0},{2,3},{3,2},{4,5},{5,4},{6,7},{7,6},{8,9},{9,8},{10,11... | collective-permute-start | bytes 2359304 | tf_op jit(solution)/shard_map/ppermute | solution.py:132
  247.7 1.9 copy-start.12
  249.6 1.9 copy-start.19
  250.7 2.1 copy-start.8
  252.8 2.0 copy-start.11
  256.1 42.4 %collective-permute-start.2 = (bf16[192,2048]{1,0:T(8,128)(2,1)S(1)}, bf16[192,2048]{1,0:T(8,128)(2,1)S(1)}, u32[]{:S(2)}, u32[]{:S(2)}) collective-permute-start(bf16[192,2048]{1,0:T(8,128)(2,1)S(1)} %constant_dynamic-slice_fusion.5), channel_id=1, source_target_pairs={{0,1},{1,0},{2,3},{3,2},{4,5},{5,4},{6,7},{7,6},{8,9},{9,8},{10,11... | collective-permute-start | bytes 2359304 | tf_op jit(solution)/shard_map/ppermute | solution.py:132
  256.3 59.1 %collective-permute-start.4 = (bf16[192,2048]{1,0:T(8,128)(2,1)S(1)}, bf16[192,2048]{1,0:T(8,128)(2,1)S(1)}, u32[]{:S(2)}, u32[]{:S(2)}) collective-permute-start(bf16[192,2048]{1,0:T(8,128)(2,1)S(1)} %constant_dynamic-slice_fusion.4), channel_id=1, source_target_pairs={{0,1},{1,0},{2,3},{3,2},{4,5},{5,4},{6,7},{7,6},{8,9},{9,8},{10,11... | collective-permute-start | bytes 2359304 | tf_op jit(solution)/shard_map/ppermute | solution.py:132
  258.2 74.0 %collective-permute-start.8 = (bf16[192,2048]{1,0:T(8,128)(2,1)S(1)}, bf16[192,2048]{1,0:T(8,128)(2,1)S(1)}, u32[]{:S(2)}, u32[]{:S(2)}) collective-permute-start(bf16[192,2048]{1,0:T(8,128)(2,1)S(1)} %constant_dynamic-slice_fusion.2), channel_id=1, source_target_pairs={{0,1},{1,0},{2,3},{3,2},{4,5},{5,4},{6,7},{7,6},{8,9},{9,8},{10,11... | collective-permute-start | bytes 2359304 | tf_op jit(solution)/shard_map/ppermute | solution.py:132
  264.8 76.5 %collective-permute-start.10 = (bf16[192,2048]{1,0:T(8,128)(2,1)S(1)}, bf16[192,2048]{1,0:T(8,128)(2,1)S(1)}, u32[]{:S(2)}, u32[]{:S(2)}) collective-permute-start(bf16[192,2048]{1,0:T(8,128)(2,1)S(1)} %constant_dynamic-slice_fusion.1), channel_id=1, source_target_pairs={{0,1},{1,0},{2,3},{3,2},{4,5},{5,4},{6,7},{7,6},{8,9},{9,8},{10,11... | collective-permute-start | bytes 2359304 | tf_op jit(solution)/shard_map/ppermute | solution.py:132
  281.6 97.5 %collective-permute-start.13 = (bf16[192,2048]{1,0:T(8,128)(2,1)S(1)}, bf16[192,2048]{1,0:T(8,128)(2,1)S(1)}, u32[]{:S(2)}, u32[]{:S(2)}) collective-permute-start(bf16[192,2048]{1,0:T(8,128)(2,1)S(1)} %add_convert_fusion.8), channel_id=1, source_target_pairs={{0,16},{4,20},{8,24},{12,28},{16,0},{20,4},{24,8},{28,12},{1,17},{... | collective-permute-start | bytes 2359304 | tf_op jit(solution)/shard_map/ppermute | solution.py:134
  298.5 54.9 %collective-permute-start.7 = (bf16[192,2048]{1,0:T(8,128)(2,1)S(1)}, bf16[192,2048]{1,0:T(8,128)(2,1)S(1)}, u32[]{:S(2)}, u32[]{:S(2)}) collective-permute-start(bf16[192,2048]{1,0:T(8,128)(2,1)S(1)} %add_convert_fusion.11), channel_id=1, source_target_pairs={{0,16},{4,20},{8,24},{12,28},{16,0},{20,4},{24,8},{28,12},{1,17},{... | collective-permute-start | bytes 2359304 | tf_op jit(solution)/shard_map/ppermute | solution.py:134
  315.3 27.2 %collective-permute-start.3 = (bf16[192,2048]{1,0:T(8,128)(2,1)S(1)}, bf16[192,2048]{1,0:T(8,128)(2,1)S(1)}, u32[]{:S(2)}, u32[]{:S(2)}) collective-permute-start(bf16[192,2048]{1,0:T(8,128)(2,1)S(1)} %add_convert_fusion.13), channel_id=1, source_target_pairs={{0,16},{4,20},{8,24},{12,28},{16,0},{20,4},{24,8},{28,12},{1,17},{... | collective-permute-start | bytes 2359304 | tf_op jit(solution)/shard_map/ppermute | solution.py:134
  332.2 20.0 %collective-permute-start.5 = (bf16[192,2048]{1,0:T(8,128)(2,1)S(1)}, bf16[192,2048]{1,0:T(8,128)(2,1)S(1)}, u32[]{:S(2)}, u32[]{:S(2)}) collective-permute-start(bf16[192,2048]{1,0:T(8,128)(2,1)S(1)} %add_convert_fusion.12), channel_id=1, source_target_pairs={{0,16},{4,20},{8,24},{12,28},{16,0},{20,4},{24,8},{28,12},{1,17},{... | collective-permute-start | bytes 2359304 | tf_op jit(solution)/shard_map/ppermute | solution.py:134
  341.3 27.8 %collective-permute-start.9 = (bf16[192,2048]{1,0:T(8,128)(2,1)S(1)}, bf16[192,2048]{1,0:T(8,128)(2,1)S(1)}, u32[]{:S(2)}, u32[]{:S(2)}) collective-permute-start(bf16[192,2048]{1,0:T(8,128)(2,1)S(1)} %add_convert_fusion.10), channel_id=1, source_target_pairs={{0,16},{4,20},{8,24},{12,28},{16,0},{20,4},{24,8},{28,12},{1,17},{... | collective-permute-start | bytes 2359304 | tf_op jit(solution)/shard_map/ppermute | solution.py:134
  342.6 35.3 %collective-permute-start.11 = (bf16[192,2048]{1,0:T(8,128)(2,1)S(1)}, bf16[192,2048]{1,0:T(8,128)(2,1)S(1)}, u32[]{:S(2)}, u32[]{:S(2)}) collective-permute-start(bf16[192,2048]{1,0:T(8,128)(2,1)S(1)} %add_convert_fusion.9), channel_id=1, source_target_pairs={{0,16},{4,20},{8,24},{12,28},{16,0},{20,4},{24,8},{28,12},{1,17},{... | collective-permute-start | bytes 2359304 | tf_op jit(solution)/shard_map/ppermute | solution.py:134
Sparse Core Ops, SparseCore 0:
  9.9 39.2 all-gather.10
  51.1 36.8 all-gather.12
  89.9 37.0 all-gather.16
  133.3 33.5 all-gather.14
  178.5 48.1 reduce-scatter.2
  230.5 53.6 reduce-scatter.4

commit v2 on v1

--- a/solution.py
+++ b/solution.py
@@ -1,10 +1,124 @@
+import functools
+
 import jax
 import jax.numpy as jnp
 from jax import lax
+from jax.experimental import pallas as pl
+from jax.experimental.pallas import tpu as pltpu
 from jax.sharding import PartitionSpec as P
 
 BF = jnp.bfloat16
 F32 = jnp.float32
+
+
+def flip(index, bit):
+    return index + bit * (1 - 2 * ((index // bit) % 2))
+
+
+def flip_all(index, mask):
+    bit = 1
+    while bit <= mask:
+        if mask & bit:
+            index = flip(index, bit)
+        bit *= 2
+    return index
+
+
+def gather_kernel(owners, n_dp, *refs):
+    ins, outs = refs[:3], refs[3:6]
+    send_sem, recv_sem, local_sem = refs[6:]
+    far = n_dp // 2
+    me = lax.axis_index("expert")
+    z = lax.axis_index("dp")
+    bits = [1 << i for i in range(1, owners.bit_length() - 1)]
+
+    barrier = pltpu.get_barrier_semaphore()
+    for bit in [1] + bits:
+        pl.semaphore_signal(
+            barrier, device_id={"expert": flip(me, bit)}, device_id_type=pl.DeviceIdType.MESH
+        )
+    for h in range(1, far):
+        pl.semaphore_signal(
+            barrier, device_id={"dp": (z + 2 * h) % n_dp}, device_id_type=pl.DeviceIdType.MESH
+        )
+    pl.semaphore_wait(barrier, len(bits) + far)
+
+    number = 0
+    started = []
+    arrival = {}
+
+    def send(src, dst, target, key):
+        nonlocal number
+        copy = pltpu.make_async_remote_copy(
+            src_ref=src,
+            dst_ref=dst,
+            send_sem=send_sem.at[number],
+            recv_sem=recv_sem.at[number],
+            device_id=target,
+            device_id_type=pl.DeviceIdType.MESH,
+        )
+        copy.start()
+        number += 1
+        started.append(copy)
+        arrival[key] = copy
+
+    landed = set()
+
+    def need(key):
+        if key in arrival and key not in landed:
+            arrival[key].wait_recv()
+            landed.add(key)
+
+    order = (2, 0, 1)
+    own = []
+    for a in order:
+        for h in range(1, far):
+            send(
+                ins[a],
+                outs[a].at[h, me],
+                {"dp": (z - 2 * h + n_dp) % n_dp},
+                (a, h, 0),
+            )
+        own.append(pltpu.make_async_copy(ins[a], outs[a].at[0, me], local_sem.at[a]))
+    ways = (bits, bits[::-1], bits[::-1])
+    for step in range(len(bits) + 1):
+        for h in range(far):
+            for a in order:
+                way = list(ways[a]) + [1]
+                bit = way[step]
+                for pick_at in range(1 << step):
+                    mask = sum(way[i] for i in range(step) if pick_at >> i & 1)
+                    need((a, h, mask))
+                    at = flip_all(me, mask)
+                    src = ins[a] if h == 0 and mask == 0 else outs[a].at[h, at]
+                    send(src, outs[a].at[h, at], {"expert": flip(me, bit)}, (a, h, mask + bit))
+        if step == 0:
+            for copy in own:
+                copy.start()
+    for key in arrival:
+        need(key)
+    for copy in started:
+        copy.wait_send()
+    for copy in own:
+        copy.wait()
+
+
+def gather(tokens, cotangent, aux, owners, n_dp):
+    far = n_dp // 2
+    copies = 3 * (far * (owners - 1) + far - 1)
+    ins = (tokens, cotangent, aux)
+    return pl.pallas_call(
+        functools.partial(gather_kernel, owners, n_dp),
+        out_shape=[jax.ShapeDtypeStruct((far, owners, *v.shape), v.dtype) for v in ins],
+        in_specs=[pl.BlockSpec(memory_space=pltpu.VMEM)] * 3,
+        out_specs=[pl.BlockSpec(memory_space=pl.ANY)] * 3,
+        scratch_shapes=[
+            pltpu.SemaphoreType.DMA((copies,)),
+            pltpu.SemaphoreType.DMA((copies,)),
+            pltpu.SemaphoreType.DMA((3,)),
+        ],
+        compiler_params=pltpu.CompilerParams(collective_id=0, has_side_effects=True),
+    )(*ins)
 
 
 def dot(a, b, dims):
@@ -56,38 +170,28 @@
     half = units // far
     part_at = (z // 2) * half
 
-    aux = jnp.concatenate([router_probs, routes.astype(F32)], axis=1).T
-    aux_all = lax.all_gather(aux, ("expert", "dp"), axis=0).reshape(owners, n_dp, 2 * top, tok)
-
-    def gathered(shift):
-        moved = (tokens, cotangent)
-        if shift:
-            pairs = [((i + shift) % n_dp, i) for i in range(n_dp)]
-            moved = tuple(lax.ppermute(v, "dp", pairs) for v in moved)
-        x_all, c_all = (lax.all_gather(v, "expert", axis=0) for v in moved)
-        own = lax.dynamic_index_in_dim(aux_all, lax.rem(z + shift, n_dp), 1, keepdims=False)
-        return x_all, c_all, own[:, :top], own[:, top:]
-
-    sets = [gathered(2 * h) for h in range(far)]
-
-    outs, dxs, chosens = [], [], []
-    pieces = []
+    spare = -(2 * top) % 8
+    aux = jnp.concatenate([router_probs.T, routes.T.astype(F32), jnp.zeros((spare, tok), F32)])
+    x_all, c_all, aux_all = gather(tokens, cotangent, aux, owners, n_dp)
+
+    picks, later, pieces = [], [], []
     for s in range(exp_dev):
         expert = (partner_here * exp_dev + s).astype(F32)
         gate_w, up_w, down_w = gate_weight[s], up_weight[s], down_weight[s]
         lists = ([], [], [])
         rows = []
-        for h, (x_all, c_all, probs, names) in enumerate(sets):
+        for h in range(far):
+            probs, names = aux_all[h, :, :top], aux_all[h, :, top : 2 * top]
             chosen, row_prob = select(names, probs, expert, capacity)
-            x = pick(chosen, x_all).astype(BF)
-            c = (pick(chosen, c_all) * row_prob).astype(BF)
+            if h == 0:
+                picks.append(chosen)
+            if pieces:
+                chosen, _ = lax.optimization_barrier((chosen, pieces[-1]))
+            x = pick(chosen, x_all[h]).astype(BF)
+            c = (pick(chosen, c_all[h]) * row_prob).astype(BF)
             if h == 0:
                 dgate, dup, hidden = acts(x, c, gate_w, up_w, down_w)
-                out = (dot(hidden, down_w, ((1,), (0,))) * row_prob).astype(BF)
-                dx = (dot(dgate, gate_w, ((1,), (1,))) + dot(dup, up_w, ((1,), (1,)))).astype(BF)
-                outs.append(out.reshape(owners, capacity, width))
-                dxs.append(dx.reshape(owners, capacity, width))
-                chosens.append(chosen)
+                later.append((dgate, dup, hidden, row_prob))
                 dgate, dup, hidden = (
                     lax.dynamic_slice_in_dim(v, part_at, half, 1) for v in (dgate, dup, hidden)
                 )
@@ -109,7 +213,15 @@
                 total = term if total is None else total + term
             pieces.append(total.astype(BF))
 
-    chosen = jnp.concatenate(chosens, axis=1)
+    chosen = jnp.concatenate(picks, axis=1)
+    outs, dxs = [], []
+    for s in range(exp_dev):
+        dgate, dup, hidden, row_prob = later[s]
+        dgate, dup, hidden, _ = lax.optimization_barrier((dgate, dup, hidden, pieces[-1]))
+        out = (dot(hidden, down_weight[s], ((1,), (0,))) * row_prob).astype(BF)
+        dx = dot(dgate, gate_weight[s], ((1,), (1,))) + dot(dup, up_weight[s], ((1,), (1,)))
+        outs.append(out.reshape(owners, capacity, width))
+        dxs.append(dx.astype(BF).reshape(owners, capacity, width))
 
     def back(values):
         stacked = jnp.concatenate(values, axis=1)

time: 402 us -> 423 us (1.052)
  Pallas kernels: 0 us -> 116 us
  blocking collectives: 81.6 us -> 0 us
  waiting for transfers between devices: 133 us -> 115 us
  other arithmetic: 15.3 us -> 23.8 us
  matrix products: 97.2 us -> 92.7 us
    pallas_call x0 -> x1, Pallas kernels: none -> 116 us  [gather(): pl.pallas_call(functools.partial(gather_kernel, owners, n_dp), out_shape=...]
    all_gather x1 -> x0, blocking collectives: 81.6 us -> none  [local(): lax.all_gather(aux, ('expert', 'dp'), axis=0)]
    ppermute x6, waiting for transfers between devices: 29.6 us -> 59.5 us  [local(): swapped = lax.ppermute(summed, 'expert', across)]
    ppermute x2 -> x0, waiting for transfers between devices: 23.4 us -> none  [gathered(): moved = tuple((lax.ppermute(v, 'dp', pairs) for v in moved))]
    ppermute x6, waiting for transfers between devices: 78.3 us -> 55.8 us  [local(): came = lax.ppermute(sent, 'dp', near)]
    dot_general x34, matrix products: 64.9 us -> 56.2 us  [dot(): return lax.dot_general(a, b, (dims, ((), ())), preferred_element_type=F32)]
    slice x3, local copies, waits for them, and re-layouts: 18.9 us -> 13 us  [local(): gate_w, up_w, down_w = (gate_weight[s], up_weight[s], down_weight[s])]
    convert_element_type x6, other arithmetic: 1.62 us -> 7.49 us  [local(): summed = (kept.astype(F32) + came.astype(F32)).astype(BF)]
  transfers between devices with their start and end apart: 20 -> 14, of which waited for: 10 -> 6; matrix products, arithmetic and copies ran while one was open for 36% -> 12% of each run, Pallas kernels for 0% -> 0%
where the time goes in v2:
time: 423 us; the launch traced here: 418 us
  Pallas kernels  116 us (27%)
  waiting for transfers between devices  115 us (27%)
  matrix products  92.7 us (22%)
  local copies, waits for them, and re-layouts  43.3 us (10%)
  other arithmetic  23.8 us (6%)
  between operations  16.3 us (4%)
  starting transfers between devices  10.4 us (2%)
    pallas_call x1, Pallas kernels, gather(): pl.pallas_call(functools.partial(gather_kernel, owners, n_dp), out_shape=...  116 us
    ppermute x6, waiting for transfers between devices, local(): swapped = lax.ppermute(summed, 'expert', across)  59.5 us
    dot_general x34, matrix products, dot(): return lax.dot_general(a, b, (dims, ((), ())), preferred_element_type=F32)  56.2 us
    ppermute x6, waiting for transfers between devices, local(): came = lax.ppermute(sent, 'dp', near)  55.8 us
    dot_general x8, matrix products, pick(): lax.dot_general(onehot, block, (((2,), (1,)), ((0,), (0,))), preferred_el...  30.5 us
    unnamed x131, local copies, waits for them, and re-layouts  23.8 us
    slice x3, local copies, waits for them, and re-layouts, local(): gate_w, up_w, down_w = (gate_weight[s], up_weight[s], down_weight[s])  13 us
  transfers between devices with their start and end apart: 14, of which 6 were waited for; matrix products, arithmetic and copies ran while one was open for 12% of the time, Pallas kernels for 0%

profile of v2, /device:TPU:0, one launch (start us, length us, event | category | flops | bytes accessed | tf_op | source)
XLA Modules:
  0.0 418.0 jit_solution(9400853431909320523)
XLA Ops:
  7.2 1.3 fusion.151
  9.9 6.4 %fusion.175 = (bf16[1,2048,768]{2,1,0:T(8,128)(2,1)}, bf16[1,2048,768]{2,1,0:T(8,128)(2,1)}) fusion(bf16[2,2048,768]{2,1,0:T(8,128)(2,1)} %param.13), kind=kLoop, calls=%fused_computation.228 | loop fusion | bytes 12582912 | tf_op jit(solution)/shard_map/slice | solution.py:180
  16.4 3.0 fusion.176
  20.1 116.1 %shard_map.103 = (bf16[2,8,128,2048]{3,2,1,0:T(8,128)(2,1)}, bf16[2,8,128,2048]{3,2,1,0:T(8,128)(2,1)}, f32[2,8,16,128]{3,2,1,0:T(8,128)}) custom-call(bf16[128,2048]{1,0:T(8,128)(2,1)} %refs_0_.1, bf16[128,2048]{1,0:T(8,128)(2,1)} %refs_1_.1, f32[16,128]{1,0:T(8,128)} %maximum_maximum_fusion.refs_2_), custom_call_target="tpu_custom_call" | custom-call | tf_op jit(solution)/shard_map/pallas_call | solution.py:110
  138.2 3.5 fusion.64
  142.3 3.0 fusion.55
  145.3 5.0 %fusion.59 = f32[512,768]{1,0:T(8,128)} fusion(bf16[512,2048]{1,0:T(8,128)(2,1)S(1)} %bitcast.183, bf16[2,2048,768]{2,1,0:T(8,128)(2,1)} %param.14), kind=kOutput, calls=%fused_computation.67 | convolution fusion | flops 1610612736 | bytes 6815744 | tf_op jit(solution)/shard_map/dot_general | solution.py:125
  150.4 2.6 fusion.70
  154.2 6.2 %multiply_convert_fusion.1 = (bf16[8,64,2048]{2,1,0:T(8,128)(2,1)}, f32[8,64,2048]{2,1,0:T(8,128)}) fusion(f32[8,64]{1,0:T(8,128)S(1)} %get-tuple-element.61, bf16[2,8,128,2048]{3,2,1,0:T(8,128)(2,1)} %get-tuple-element.15, f32[8,128]{1,0:T(8,128)S(1)} %convolution_add_fusion.1, pred[8,128]{1,0:T(8,128)(4,1)S(1)} %get-tuple-element.34), kind=kOutput, calls=%fused_computation.33 | convolution fusion | flops 270663680 | bytes 10492928 | tf_op jit(solution)/shard_map/dot_general | solution.py:129
  161.6 6.2 %multiply_convert_fusion.5 = (bf16[8,64,2048]{2,1,0:T(8,128)(2,1)}, f32[8,64,2048]{2,1,0:T(8,128)}) fusion(f32[8,64]{1,0:T(8,128)S(1)} %get-tuple-element.63, bf16[2,8,128,2048]{3,2,1,0:T(8,128)(2,1)} %get-tuple-element.15, f32[8,128]{1,0:T(8,128)S(1)} %convolution_add_fusion.3, pred[8,128]{1,0:T(8,128)(4,1)S(1)} %reduce_or.36), kind=kOutput, calls=%fused_computation.39 | convolution fusion | flops 270663680 | bytes 10492928 | tf_op jit(solution)/shard_map/dot_general | solution.py:129
  168.3 3.4 fusion.90
  171.9 1.2 fusion.88
  173.1 1.2 copy-done.3
  174.6 1.9 copy-done.4
  178.2 5.6 %multiply_convert_fusion.10 = (bf16[512,768]{1,0:T(8,128)(2,1)}, bf16[512,768]{1,0:T(8,128)(2,1)}, bf16[512,768]{1,0:T(8,128)(2,1)S(1)}) fusion(f32[512,768]{1,0:T(8,128)S(1)} %copy-done.47, f32[512,768]{1,0:T(8,128)S(1)} %copy-done.48, bf16[512,2048]{1,0:T(8,128)(2,1)S(1)} %bitcast.215, bf16[2,768,2048]{2,1,0:T(8,128)(2,1)} %param.15), kind=kOutput, calls=%fused_computation.112 | convolution fusion | flops 1616510976 | bytes 10747904 | tf_op jit(solution)/shard_map/dot_general | solution.py:125
  184.9 2.4 add_convert_fusion.7
  187.3 2.1 fusion.73
  189.4 3.6 multiply_convert_fusion
  194.2 3.2 multiply_convert_fusion.3
  197.4 3.1 fusion.67
  200.6 1.3 fusion.86
  201.9 1.6 copy-done.14
  203.5 1.3 fusion.84
  204.8 1.8 fusion.43
  206.9 1.8 fusion.51
  211.2 2.2 multiply_convert_fusion.8
  214.4 2.3 add_convert_fusion.6
  216.7 1.8 fusion.53
  218.6 2.0 fusion.45
  220.6 1.9 add_convert_fusion.1
  222.5 1.8 add_convert_fusion
  224.3 2.9 fusion.28
  227.4 2.1 constant_dynamic-slice_fusion
  229.5 3.6 fusion.174
  233.1 1.3 fusion.80
  239.1 1.9 collective-permute-start.8
  242.1 1.2 add_convert_fusion.3
  244.7 1.3 fusion.82
  250.5 1.7 collective-permute-start.2
  252.2 1.8 multiply_convert_fusion.4
  254.0 1.8 multiply_convert_fusion.2
  255.8 3.2 fusion.31
  259.0 1.1 copy-done.35
  262.4 1.2 add_convert_fusion.5
  265.5 1.8 collective-permute-start.4
  267.3 1.6 add_convert_fusion.8
  269.8 1.4 add_convert_fusion.9
  271.2 12.7 %collective-permute-done.6 = bf16[192,2048]{1,0:T(8,128)(2,1)} collective-permute-done((bf16[192,2048]{1,0:T(8,128)(2,1)}, bf16[192,2048]{1,0:T(8,128)(2,1)}, u32[]{:S(2)}, u32[]{:S(2)}) %collective-permute-start.6) | collective-permute-done | bytes 786464 | tf_op jit(solution)/shard_map/ppermute | solution.py:244
  284.4 1.4 add_convert_fusion.10
  285.9 31.8 %collective-permute-done = bf16[192,2048]{1,0:T(8,128)(2,1)} collective-permute-done((bf16[192,2048]{1,0:T(8,128)(2,1)}, bf16[192,2048]{1,0:T(8,128)(2,1)}, u32[]{:S(2)}, u32[]{:S(2)}) %collective-permute-start) | collective-permute-done | bytes 786464 | tf_op jit(solution)/shard_map/ppermute | solution.py:244
  318.2 1.4 add_convert_fusion.13
  319.6 1.6 collective-permute-start.1
  321.1 1.4 add_convert_fusion.12
  322.5 11.3 %collective-permute-done.4 = bf16[192,2048]{1,0:T(8,128)(2,1)S(1)} collective-permute-done((bf16[192,2048]{1,0:T(8,128)(2,1)S(1)}, bf16[192,2048]{1,0:T(8,128)(2,1)S(1)}, u32[]{:S(2)}, u32[]{:S(2)}) %collective-permute-start.4) | collective-permute-done | bytes 786464 | tf_op jit(solution)/shard_map/ppermute | solution.py:244
  334.6 29.1 %collective-permute-done.1 = bf16[192,2048]{1,0:T(8,128)(2,1)S(1)} collective-permute-done((bf16[192,2048]{1,0:T(8,128)(2,1)S(1)}, bf16[192,2048]{1,0:T(8,128)(2,1)S(1)}, u32[]{:S(2)}, u32[]{:S(2)}) %collective-permute-start.1) | collective-permute-done | bytes 786464 | tf_op jit(solution)/shard_map/ppermute | solution.py:246
  364.1 1.2 bitcast_dynamic-update-slice_fusion.5
  365.3 15.3 %collective-permute-done.3 = bf16[192,2048]{1,0:T(8,128)(2,1)S(1)} collective-permute-done((bf16[192,2048]{1,0:T(8,128)(2,1)S(1)}, bf16[192,2048]{1,0:T(8,128)(2,1)S(1)}, u32[]{:S(2)}, u32[]{:S(2)}) %collective-permute-start.3) | collective-permute-done | bytes 786464 | tf_op jit(solution)/shard_map/ppermute | solution.py:246
  380.6 1.2 bitcast_dynamic-update-slice_fusion.4
  381.8 15.1 %collective-permute-done.5 = bf16[192,2048]{1,0:T(8,128)(2,1)S(1)} collective-permute-done((bf16[192,2048]{1,0:T(8,128)(2,1)S(1)}, bf16[192,2048]{1,0:T(8,128)(2,1)S(1)}, u32[]{:S(2)}, u32[]{:S(2)}) %collective-permute-start.5) | collective-permute-done | bytes 786464 | tf_op jit(solution)/shard_map/ppermute | solution.py:246
  396.9 1.2 bitcast_dynamic-update-slice_fusion.3
  398.0 1.2 bitcast_dynamic-update-slice_fusion.2
  399.2 1.2 bitcast_dynamic-update-slice_fusion.1
  400.4 1.2 bitcast_dynamic-update-slice_fusion
  401.6 9.4 %copy.19 = bf16[192,2,3,2048]{3,1,2,0:T(2,128)(2,1)} copy(bf16[192,2,3,2048]{3,0,2,1:T(8,128)(2,1)} %bitcast.42) | data formatting | bytes 9437184
  (192 shorter events, 33.6 us)
Async XLA Ops:
  7.2 403.8 %reduce-scatter.5.cloned.1.call-start = ((), (), s32[]{:S(2)}) async-start(), calls=%async_computation.3 | async-start | bytes 4718592 | tf_op jit(solution)/shard_map/reduce_scatter | solution.py:231
  9.1 7.3 %slice-start.6 = ((s8[6291456]{0:T(1024)(128)(4,1)}), s8[4194304]{0:T(1024)(128)(4,1)S(1)}, s32[]{:S(2)}) async-start(s8[6291456]{0:T(1024)(128)(4,1)} %bitcast.198), calls=%async_computation.10 | async-start | bytes 8388608
  9.9 6.4 %slice-start.7 = ((s8[6291456]{0:T(1024)(128)(4,1)}), s8[2097152]{0:T(1024)(128)(4,1)S(1)}, s32[]{:S(2)}) async-start(s8[6291456]{0:T(1024)(128)(4,1)} %bitcast.198), calls=%async_computation.11 | async-start | bytes 4194304
  16.3 3.1 copy-start.46
  138.2 4.1 copy-start.12
  142.3 8.1 %slice-start.2 = ((s8[8388608]{0:T(1024)(128)(4,1)}), s8[4194304]{0:T(1024)(128)(4,1)S(1)}, s32[]{:S(2)}) async-start(s8[8388608]{0:T(1024)(128)(4,1)} %bitcast.178), calls=%async_computation.6 | async-start | bytes 8388608
  145.3 5.1 %slice-start.3 = ((s8[8388608]{0:T(1024)(128)(4,1)}), s8[4194304]{0:T(1024)(128)(4,1)S(1)}, s32[]{:S(2)}) async-start(s8[8388608]{0:T(1024)(128)(4,1)} %bitcast.178), calls=%async_computation.7 | async-start | bytes 8388608
  168.2 3.5 copy-start.5
  168.2 3.6 copy-start.15
  171.7 75.4 %copy-start.24 = (f32[512,384]{1,0:T(8,128)}, f32[512,384]{1,0:T(8,128)S(1)}, u32[]{:S(2)}) copy-start(f32[512,384]{1,0:T(8,128)S(1)} %fusion.90) | copy-start | bytes 2359300
  171.7 2.6 copy-start.3
  171.9 5.0 %copy-start.48 = (f32[512,768]{1,0:T(8,128)S(1)}, f32[512,768]{1,0:T(8,128)}, u32[]{:S(2)}) copy-start(f32[512,768]{1,0:T(8,128)} %fusion.59) | copy-start | bytes 4718596
  173.1 11.7 %copy-start.26 = (f32[512,384]{1,0:T(8,128)}, f32[512,384]{1,0:T(8,128)S(1)}, u32[]{:S(2)}) copy-start(f32[512,384]{1,0:T(8,128)S(1)} %fusion.88) | copy-start | bytes 2359300
  174.3 2.2 copy-start.4
  174.3 2.8 copy-start.47
  176.5 10.7 %slice-start.4 = ((s8[8388608]{0:T(1024)(128)(4,1)}), s8[4194304]{0:T(1024)(128)(4,1)S(1)}, s32[]{:S(2)}) async-start(s8[8388608]{0:T(1024)(128)(4,1)} %bitcast.180), calls=%async_computation.8 | async-start | bytes 8388608
  178.2 9.0 %slice-start.5 = ((s8[8388608]{0:T(1024)(128)(4,1)}), s8[4194304]{0:T(1024)(128)(4,1)S(1)}, s32[]{:S(2)}) async-start(s8[8388608]{0:T(1024)(128)(4,1)} %bitcast.180), calls=%async_computation.9 | async-start | bytes 8388608
  183.8 3.4 copy-start.36
  183.8 5.5 %slice-start = ((s8[8388608]{0:T(1024)(128)(4,1)}), s8[4194304]{0:T(1024)(128)(4,1)S(1)}, s32[]{:S(2)}) async-start(s8[8388608]{0:T(1024)(128)(4,1)} %bitcast.176), calls=%async_computation.4 | async-start | bytes 8388608
  184.9 4.5 %slice-start.1 = ((s8[8388608]{0:T(1024)(128)(4,1)}), s8[4194304]{0:T(1024)(128)(4,1)S(1)}, s32[]{:S(2)}) async-start(s8[8388608]{0:T(1024)(128)(4,1)} %bitcast.176), calls=%async_computation.5 | async-start | bytes 8388608
  194.2 6.3 %copy-start.13 = (bf16[1,2048,768]{2,1,0:T(8,128)(2,1)S(1)}, bf16[1,2048,768]{2,1,0:T(8,128)(2,1)}, u32[]{:S(2)}) copy-start(bf16[1,2048,768]{2,1,0:T(8,128)(2,1)} %get-tuple-element.40) | copy-start | bytes 9437188
  197.4 3.2 copy-start.8
  197.4 7.3 %slice-start.12 = ((s8[6291456]{0:T(1024)(128)(4,1)}), s8[4194304]{0:T(1024)(128)(4,1)S(1)}, s32[]{:S(2)}) async-start(s8[6291456]{0:T(1024)(128)(4,1)} %bitcast.204), calls=%async_computation.16 | async-start | bytes 8388608
  200.6 9.1 %copy-start = (bf16[8,64,2048]{2,1,0:T(8,128)(2,1)}, bf16[8,64,2048]{2,1,0:T(8,128)(2,1)S(1)}, u32[]{:S(2)}) copy-start(bf16[8,64,2048]{2,1,0:T(8,128)(2,1)S(1)} %fusion.67) | copy-start | bytes 6291460
  200.6 2.9 copy-start.14
  200.6 4.2 %slice-start.13 = ((s8[6291456]{0:T(1024)(128)(4,1)}), s8[2097152]{0:T(1024)(128)(4,1)S(1)}, s32[]{:S(2)}) async-start(s8[6291456]{0:T(1024)(128)(4,1)} %bitcast.204), calls=%async_computation.17 | async-start | bytes 4194304
  201.9 12.6 %copy-start.28 = (f32[512,384]{1,0:T(8,128)}, f32[512,384]{1,0:T(8,128)S(1)}, u32[]{:S(2)}) copy-start(f32[512,384]{1,0:T(8,128)S(1)} %fusion.86) | copy-start | bytes 2359300
  203.5 3.2 slice-start.10
  204.8 9.7 %copy-start.30 = (f32[512,384]{1,0:T(8,128)}, f32[512,384]{1,0:T(8,128)S(1)}, u32[]{:S(2)}) copy-start(f32[512,384]{1,0:T(8,128)S(1)} %fusion.84) | copy-start | bytes 2359300
  206.9 2.2 copy-start.2
  206.9 3.5 slice-start.8
  213.4 3.4 copy-start.40
  213.4 5.2 %copy-start.44 = (bf16[512,768]{1,0:T(8,128)(2,1)}, bf16[512,768]{1,0:T(8,128)(2,1)S(1)}, u32[]{:S(2)}) copy-start(bf16[512,768]{1,0:T(8,128)(2,1)S(1)} %get-tuple-element.24) | copy-start | bytes 2359300
  213.4 9.1 %copy-start.42 = (bf16[512,768]{1,0:T(8,128)(2,1)}, bf16[512,768]{1,0:T(8,128)(2,1)S(1)}, u32[]{:S(2)}) copy-start(bf16[512,768]{1,0:T(8,128)(2,1)S(1)} %get-tuple-element.23) | copy-start | bytes 2359300
  214.4 2.3 copy-start.34
  227.3 183.6 %reduce-scatter.3.cloned.1.call-start = ((), (), s32[]{:S(2)}) async-start(), calls=%async_computation.2 | async-start | bytes 4718592 | tf_op jit(solution)/shard_map/reduce_scatter | solution.py:231
  229.5 3.6 copy-start.16
  229.5 36.0 %collective-permute-start.10 = (bf16[192,2048]{1,0:T(8,128)(2,1)}, bf16[192,2048]{1,0:T(8,128)(2,1)}, u32[]{:S(2)}, u32[]{:S(2)}) collective-permute-start(bf16[192,2048]{1,0:T(8,128)(2,1)} %constant_dynamic-slice_fusion), channel_id=1, source_target_pairs={{0,1},{1,0},{2,3},{3,2},{4,5},{5,4},{6,7},{7,6},{8,9},{9,8},{10,11... | collective-permute-start | bytes 2359304 | tf_op jit(solution)/shard_map/ppermute | solution.py:244
  237.0 4.0 copy-start.43
  238.1 2.9 copy-start.22
  239.1 2.9 copy-start.31
  239.1 29.9 %collective-permute-start.8 = (bf16[192,2048]{1,0:T(8,128)(2,1)}, bf16[192,2048]{1,0:T(8,128)(2,1)}, u32[]{:S(2)}, u32[]{:S(2)}) collective-permute-start(bf16[192,2048]{1,0:T(8,128)(2,1)} %constant_dynamic-slice_fusion.1), channel_id=1, source_target_pairs={{0,1},{1,0},{2,3},{3,2},{4,5},{5,4},{6,7},{7,6},{8,9},{9,8},{10,11... | collective-permute-start | bytes 2359304 | tf_op jit(solution)/shard_map/ppermute | solution.py:244
  242.1 2.7 copy-start.17
  243.3 2.8 copy-start.10
  244.3 39.6 %collective-permute-start.6 = (bf16[192,2048]{1,0:T(8,128)(2,1)}, bf16[192,2048]{1,0:T(8,128)(2,1)}, u32[]{:S(2)}, u32[]{:S(2)}) collective-permute-start(bf16[192,2048]{1,0:T(8,128)(2,1)} %constant_dynamic-slice_fusion.2), channel_id=1, source_target_pairs={{0,1},{1,0},{2,3},{3,2},{4,5},{5,4},{6,7},{7,6},{8,9},{9,8},{10,11... | collective-permute-start | bytes 2359304 | tf_op jit(solution)/shard_map/ppermute | solution.py:244
  246.1 3.0 copy-start.32
  246.1 6.1 %slice-start.14 = ((s8[6291456]{0:T(1024)(128)(4,1)}), s8[4194304]{0:T(1024)(128)(4,1)S(1)}, s32[]{:S(2)}) async-start(s8[6291456]{0:T(1024)(128)(4,1)} %bitcast.206), calls=%async_computation.18 | async-start | bytes 8388608
  247.9 4.2 %slice-start.15 = ((s8[6291456]{0:T(1024)(128)(4,1)}), s8[2097152]{0:T(1024)(128)(4,1)S(1)}, s32[]{:S(2)}) async-start(s8[6291456]{0:T(1024)(128)(4,1)} %bitcast.206), calls=%async_computation.19 | async-start | bytes 4194304
  248.0 4.2 %copy-start.37 = (bf16[512,768]{1,0:T(8,128)(2,1)S(1)}, bf16[512,768]{1,0:T(8,128)(2,1)}, u32[]{:S(2)}) copy-start(bf16[512,768]{1,0:T(8,128)(2,1)} %copy-done.36) | copy-start | bytes 2359300
  250.5 3.5 copy-start.41
  250.5 69.1 %collective-permute-start.2 = (bf16[192,2048]{1,0:T(8,128)(2,1)}, bf16[192,2048]{1,0:T(8,128)(2,1)}, u32[]{:S(2)}, u32[]{:S(2)}) collective-permute-start(bf16[192,2048]{1,0:T(8,128)(2,1)} %constant_dynamic-slice_fusion.4), channel_id=1, source_target_pairs={{0,1},{1,0},{2,3},{3,2},{4,5},{5,4},{6,7},{7,6},{8,9},{9,8},{10,11... | collective-permute-start | bytes 2359304 | tf_op jit(solution)/shard_map/ppermute | solution.py:244
  260.1 2.3 copy-start.33
  262.4 3.0 copy-start.19
  264.6 53.1 %collective-permute-start = (bf16[192,2048]{1,0:T(8,128)(2,1)}, bf16[192,2048]{1,0:T(8,128)(2,1)}, u32[]{:S(2)}, u32[]{:S(2)}) collective-permute-start(bf16[192,2048]{1,0:T(8,128)(2,1)} %constant_dynamic-slice_fusion.5), channel_id=1, source_target_pairs={{0,1},{1,0},{2,3},{3,2},{4,5},{5,4},{6,7},{7,6},{8,9},{9,8},{10,11... | collective-permute-start | bytes 2359304 | tf_op jit(solution)/shard_map/ppermute | solution.py:244
  265.4 4.4 %copy-start.23 = (bf16[384,2048]{1,0:T(8,128)(2,1)S(1)}, bf16[384,2048]{1,0:T(8,128)(2,1)}, u32[]{:S(2)}) copy-start(bf16[384,2048]{1,0:T(8,128)(2,1)} %copy-done.22) | copy-start | bytes 4718596
  265.4 19.0 %copy-start.11 = (bf16[384,2048]{1,0:T(8,128)(2,1)S(1)}, bf16[384,2048]{1,0:T(8,128)(2,1)}, u32[]{:S(2)}) copy-start(bf16[384,2048]{1,0:T(8,128)(2,1)} %copy-done.10) | copy-start | bytes 4718596
  265.5 68.3 %collective-permute-start.4 = (bf16[192,2048]{1,0:T(8,128)(2,1)S(1)}, bf16[192,2048]{1,0:T(8,128)(2,1)S(1)}, u32[]{:S(2)}, u32[]{:S(2)}) collective-permute-start(bf16[192,2048]{1,0:T(8,128)(2,1)S(1)} %constant_dynamic-slice_fusion.3), channel_id=1, source_target_pairs={{0,1},{1,0},{2,3},{3,2},{4,5},{5,4},{6,7},{7,6},{8,9},{9,8},{10,11... | collective-permute-start | bytes 2359304 | tf_op jit(solution)/shard_map/ppermute | solution.py:244
  269.0 52.2 %copy-start.21 = (bf16[384,2048]{1,0:T(8,128)(2,1)S(1)}, bf16[384,2048]{1,0:T(8,128)(2,1)}, u32[]{:S(2)}) copy-start(bf16[384,2048]{1,0:T(8,128)(2,1)} %copy-done.20) | copy-start | bytes 4718596
  269.0 131.4 %collective-permute-start.11 = (bf16[192,2048]{1,0:T(8,128)(2,1)S(1)}, bf16[192,2048]{1,0:T(8,128)(2,1)S(1)}, u32[]{:S(2)}, u32[]{:S(2)}) collective-permute-start(bf16[192,2048]{1,0:T(8,128)(2,1)S(1)} %add_convert_fusion.8), channel_id=1, source_target_pairs={{0,16},{4,20},{8,24},{12,28},{16,0},{20,4},{24,8},{28,12},{1,17},{... | collective-permute-start | bytes 2359304 | tf_op jit(solution)/shard_map/ppermute | solution.py:246
  283.9 115.3 %collective-permute-start.9 = (bf16[192,2048]{1,0:T(8,128)(2,1)S(1)}, bf16[192,2048]{1,0:T(8,128)(2,1)S(1)}, u32[]{:S(2)}, u32[]{:S(2)}) collective-permute-start(bf16[192,2048]{1,0:T(8,128)(2,1)S(1)} %add_convert_fusion.9), channel_id=1, source_target_pairs={{0,16},{4,20},{8,24},{12,28},{16,0},{20,4},{24,8},{28,12},{1,17},{... | collective-permute-start | bytes 2359304 | tf_op jit(solution)/shard_map/ppermute | solution.py:246
  317.6 80.4 %collective-permute-start.7 = (bf16[192,2048]{1,0:T(8,128)(2,1)S(1)}, bf16[192,2048]{1,0:T(8,128)(2,1)S(1)}, u32[]{:S(2)}, u32[]{:S(2)}) collective-permute-start(bf16[192,2048]{1,0:T(8,128)(2,1)S(1)} %add_convert_fusion.10), channel_id=1, source_target_pairs={{0,16},{4,20},{8,24},{12,28},{16,0},{20,4},{24,8},{28,12},{1,17},{... | collective-permute-start | bytes 2359304 | tf_op jit(solution)/shard_map/ppermute | solution.py:246
  319.6 44.2 %collective-permute-start.1 = (bf16[192,2048]{1,0:T(8,128)(2,1)S(1)}, bf16[192,2048]{1,0:T(8,128)(2,1)S(1)}, u32[]{:S(2)}, u32[]{:S(2)}) collective-permute-start(bf16[192,2048]{1,0:T(8,128)(2,1)S(1)} %add_convert_fusion.13), channel_id=1, source_target_pairs={{0,16},{4,20},{8,24},{12,28},{16,0},{20,4},{24,8},{28,12},{1,17},{... | collective-permute-start | bytes 2359304 | tf_op jit(solution)/shard_map/ppermute | solution.py:246
  333.8 46.7 %collective-permute-start.3 = (bf16[192,2048]{1,0:T(8,128)(2,1)S(1)}, bf16[192,2048]{1,0:T(8,128)(2,1)S(1)}, u32[]{:S(2)}, u32[]{:S(2)}) collective-permute-start(bf16[192,2048]{1,0:T(8,128)(2,1)S(1)} %add_convert_fusion.12), channel_id=1, source_target_pairs={{0,16},{4,20},{8,24},{12,28},{16,0},{20,4},{24,8},{28,12},{1,17},{... | collective-permute-start | bytes 2359304 | tf_op jit(solution)/shard_map/ppermute | solution.py:246
  363.7 33.1 %collective-permute-start.5 = (bf16[192,2048]{1,0:T(8,128)(2,1)S(1)}, bf16[192,2048]{1,0:T(8,128)(2,1)S(1)}, u32[]{:S(2)}, u32[]{:S(2)}) collective-permute-start(bf16[192,2048]{1,0:T(8,128)(2,1)S(1)} %add_convert_fusion.11), channel_id=1, source_target_pairs={{0,16},{4,20},{8,24},{12,28},{16,0},{20,4},{24,8},{28,12},{1,17},{... | collective-permute-start | bytes 2359304 | tf_op jit(solution)/shard_map/ppermute | solution.py:246
  (15 other events, 26.8 us)
Sparse Core Ops, SparseCore 0:
  227.4 56.9 reduce-scatter.4
  288.3 60.9 reduce-scatter.2

commit v3 on v2

--- a/solution.py
+++ b/solution.py
@@ -81,20 +81,46 @@
             )
         own.append(pltpu.make_async_copy(ins[a], outs[a].at[0, me], local_sem.at[a]))
     ways = (bits, bits[::-1], bits[::-1])
-    for step in range(len(bits) + 1):
-        for h in range(far):
+    depth = len(bits)
+
+    def forward(a, h, mask, bit):
+        need((a, h, mask))
+        at = flip_all(me, mask)
+        src = ins[a] if h == 0 and mask == 0 else outs[a].at[h, at]
+        send(src, outs[a].at[h, at], {"expert": flip(me, bit)}, (a, h, mask + bit))
+
+    def masks(a, lo, hi):
+        way = ways[a]
+        return [sum(way[i] for i in range(depth) if p >> i & 1) for p in range(lo, hi)]
+
+    def spread(h, a, step):
+        for mask in masks(a, 0, 1 << step):
+            forward(a, h, mask, ways[a][step])
+
+    def sibling(h, a, step):
+        for mask in masks(a, (1 << step) // 2, 1 << step):
+            forward(a, h, mask, 1)
+
+    for step in range(depth):
+        for a in order:
+            spread(0, a, step)
+        for a in order:
+            sibling(0, a, step)
+    for copy in own:
+        copy.start()
+    for h in range(1, far):
+        for a in order:
+            spread(h, a, 0)
+            sibling(h, a, 0)
+    for a in order:
+        sibling(0, a, depth)
+    for h in range(1, far):
+        for step in range(1, depth):
             for a in order:
-                way = list(ways[a]) + [1]
-                bit = way[step]
-                for pick_at in range(1 << step):
-                    mask = sum(way[i] for i in range(step) if pick_at >> i & 1)
-                    need((a, h, mask))
-                    at = flip_all(me, mask)
-                    src = ins[a] if h == 0 and mask == 0 else outs[a].at[h, at]
-                    send(src, outs[a].at[h, at], {"expert": flip(me, bit)}, (a, h, mask + bit))
-        if step == 0:
-            for copy in own:
-                copy.start()
+                spread(h, a, step)
+                sibling(h, a, step)
+        for a in order:
+            sibling(h, a, depth)
     for key in arrival:
         need(key)
     for copy in started:
@@ -174,7 +200,11 @@
     aux = jnp.concatenate([router_probs.T, routes.T.astype(F32), jnp.zeros((spare, tok), F32)])
     x_all, c_all, aux_all = gather(tokens, cotangent, aux, owners, n_dp)
 
-    picks, later, pieces = [], [], []
+    quarter = half // 2
+    mine = lax.rem(z, 2)
+    near = [(i, i ^ 1) for i in range(n_dp)]
+    across = [(i, i ^ (owners // 2)) for i in range(owners)]
+    picks, later, pieces, sums = [], [], [], []
     for s in range(exp_dev):
         expert = (partner_here * exp_dev + s).astype(F32)
         gate_w, up_w, down_w = gate_weight[s], up_weight[s], down_weight[s]
@@ -186,7 +216,7 @@
             if h == 0:
                 picks.append(chosen)
             if pieces:
-                chosen, _ = lax.optimization_barrier((chosen, pieces[-1]))
+                chosen, _ = lax.optimization_barrier((chosen, tuple(pieces)))
             x = pick(chosen, x_all[h]).astype(BF)
             c = (pick(chosen, c_all[h]) * row_prob).astype(BF)
             if h == 0:
@@ -211,13 +241,19 @@
             for h in range(far):
                 term = dot(lists[m][h], rows[h][m], ((0,), (0,)))
                 total = term if total is None else total + term
-            pieces.append(total.astype(BF))
+            piece = total.astype(BF)
+            pieces.append(piece)
+            kept = lax.dynamic_slice_in_dim(piece, mine * quarter, quarter, 0)
+            sent = lax.dynamic_slice_in_dim(piece, (1 - mine) * quarter, quarter, 0)
+            came = lax.ppermute(sent, "dp", near)
+            sums.append((kept.astype(F32) + came.astype(F32)).astype(BF))
 
     chosen = jnp.concatenate(picks, axis=1)
     outs, dxs = [], []
     for s in range(exp_dev):
         dgate, dup, hidden, row_prob = later[s]
-        dgate, dup, hidden, _ = lax.optimization_barrier((dgate, dup, hidden, pieces[-1]))
+        hidden, _ = lax.optimization_barrier((hidden, (*pieces, *sums[:3])))
+        dgate, dup, _ = lax.optimization_barrier((dgate, dup, tuple(sums)))
         out = (dot(hidden, down_weight[s], ((1,), (0,))) * row_prob).astype(BF)
         dx = dot(dgate, gate_weight[s], ((1,), (1,))) + dot(dup, up_weight[s], ((1,), (1,)))
         outs.append(out.reshape(owners, capacity, width))
@@ -233,16 +269,8 @@
     output = back(outs)
     token_grad = back(dxs)
 
-    quarter = half // 2
-    mine = lax.rem(z, 2)
-    near = [(i, i ^ 1) for i in range(n_dp)]
-    across = [(i, i ^ (owners // 2)) for i in range(owners)]
     finished = []
-    for piece in pieces:
-        kept = lax.dynamic_slice_in_dim(piece, mine * quarter, quarter, 0)
-        sent = lax.dynamic_slice_in_dim(piece, (1 - mine) * quarter, quarter, 0)
-        came = lax.ppermute(sent, "dp", near)
-        summed = (kept.astype(F32) + came.astype(F32)).astype(BF)
+    for summed in sums:
         swapped = lax.ppermute(summed, "expert", across)
         finished.append(jnp.where(partner_here == row_here, summed, swapped))
     grads = jnp.stack(finished, axis=1).reshape(quarter, exp_dev, 3, width)

time: 423 us -> 457 us (1.080)
  waiting for transfers between devices: 115 us -> 152 us
  Pallas kernels: 116 us -> 92.2 us
  matrix products: 92.7 us -> 104 us
  other arithmetic: 23.8 us -> 32.6 us
    ppermute x6, waiting for transfers between devices: 59.5 us -> 105 us  [local(): swapped = lax.ppermute(summed, 'expert', across)]
    pallas_call x1, Pallas kernels: 116 us -> 92.2 us  [gather(): pl.pallas_call(functools.partial(gather_kernel, owners, n_dp), out_shape=...]
    dot_general x34, matrix products: 56.2 us -> 67.5 us  [dot(): return lax.dot_general(a, b, (dims, ((), ())), preferred_element_type=F32)]
    ppermute x6, waiting for transfers between devices: 55.8 us -> 46.5 us  [local(): came = lax.ppermute(sent, 'dp', near)]
    unnamed x131 -> x137, local copies, waits for them, and re-layouts: 23.8 us -> 25.8 us
  transfers between devices with their start and end apart: 14 -> 14, of which waited for: 6 -> 9; matrix products, arithmetic and copies ran while one was open for 12% -> 21% of each run, Pallas kernels for 0% -> 0%
where the time goes in v3:
time: 457 us; the launch traced here: 450 us
  waiting for transfers between devices  152 us (33%)
  matrix products  104 us (23%)
  Pallas kernels  92.2 us (20%)
  local copies, waits for them, and re-layouts  43.6 us (10%)
  other arithmetic  32.6 us (7%)
  between operations  16.2 us (4%)
  starting transfers between devices  10.5 us (2%)
    ppermute x6, waiting for transfers between devices, local(): swapped = lax.ppermute(summed, 'expert', across)  105 us
    pallas_call x1, Pallas kernels, gather(): pl.pallas_call(functools.partial(gather_kernel, owners, n_dp), out_shape=...  92.2 us
    dot_general x34, matrix products, dot(): return lax.dot_general(a, b, (dims, ((), ())), preferred_element_type=F32)  67.5 us
    ppermute x6, waiting for transfers between devices, local(): came = lax.ppermute(sent, 'dp', near)  46.5 us
    dot_general x8, matrix products, pick(): lax.dot_general(onehot, block, (((2,), (1,)), ((0,), (0,))), preferred_el...  29.8 us
    unnamed x137, local copies, waits for them, and re-layouts  25.8 us
    slice x3, local copies, waits for them, and re-layouts, local(): gate_w, up_w, down_w = (gate_weight[s], up_weight[s], down_weight[s])  13.1 us
    convert_element_type x6, other arithmetic, local(): sums.append((kept.astype(F32) + came.astype(F32)).astype(BF))  9.66 us
  transfers between devices with their start and end apart: 14, of which 9 were waited for; matrix products, arithmetic and copies ran while one was open for 21% of the time, Pallas kernels for 0%

profile of v3, /device:TPU:0, one launch (start us, length us, event | category | flops | bytes accessed | tf_op | source)
XLA Modules:
  0.0 450.2 jit_solution(16719139089959356488)
XLA Ops:
  7.2 1.4 fusion.151
  10.0 1.4 maximum_maximum_fusion.refs_2_
  11.3 92.2 %shard_map.103 = (bf16[2,8,128,2048]{3,2,1,0:T(8,128)(2,1)}, bf16[2,8,128,2048]{3,2,1,0:T(8,128)(2,1)}, f32[2,8,16,128]{3,2,1,0:T(8,128)}) custom-call(bf16[128,2048]{1,0:T(8,128)(2,1)} %refs_0_.1, bf16[128,2048]{1,0:T(8,128)(2,1)} %refs_1_.1, f32[16,128]{1,0:T(8,128)} %maximum_maximum_fusion.refs_2_), custom_call_target="tpu_custom_call" | custom-call | tf_op jit(solution)/shard_map/pallas_call | solution.py:136
  105.6 6.6 %fusion.176 = (bf16[1,2048,768]{2,1,0:T(8,128)(2,1)}, bf16[1,2048,768]{2,1,0:T(8,128)(2,1)}) fusion(bf16[2,2048,768]{2,1,0:T(8,128)(2,1)} %param.13), kind=kLoop, calls=%fused_computation.229 | loop fusion | bytes 12582912 | tf_op jit(solution)/shard_map/slice | solution.py:210
  112.9 1.4 fusion.64
  114.9 3.0 fusion.62
  118.0 3.4 fusion.175
  122.4 2.9 multiply_convert_fusion.5
  125.2 3.0 fusion.54
  128.4 4.8 %fusion.70 = bf16[8,64,2048]{2,1,0:T(8,128)(2,1)} fusion(bf16[2,8,128,2048]{3,2,1,0:T(8,128)(2,1)} %get-tuple-element.15, f32[8,128]{1,0:T(8,128)S(1)} %convolution_add_fusion.1, pred[8,128]{1,0:T(8,128)(4,1)S(1)} %get-tuple-element.34), kind=kOutput, calls=%fused_computation.80 | convolution fusion | flops 269615104 | bytes 6296576 | tf_op jit(solution)/shard_map/dot_general | solution.py:155
  133.4 1.5 select_reduce_fusion
  135.0 6.3 %multiply_convert_fusion.4 = (bf16[8,64,2048]{2,1,0:T(8,128)(2,1)}, f32[8,64,2048]{2,1,0:T(8,128)}) fusion(f32[8,64]{1,0:T(8,128)S(1)} %get-tuple-element.61, bf16[2,8,128,2048]{3,2,1,0:T(8,128)(2,1)} %get-tuple-element.16, f32[8,128]{1,0:T(8,128)S(1)} %convolution_add_fusion.1, pred[8,128]{1,0:T(8,128)(4,1)S(1)} %get-tuple-element.34), kind=kOutput, calls=%fused_computation.38 | convolution fusion | flops 270663680 | bytes 10492928 | tf_op jit(solution)/shard_map/dot_general | solution.py:155
  141.3 3.1 fusion.174
  144.4 3.4 multiply_convert_fusion.11
  147.8 2.7 fusion.125
  150.5 1.2 copy-done.19
  151.7 1.2 fusion.86
  153.0 2.1 fusion.88
  155.8 2.2 fusion.90
  158.0 4.2 add_convert_fusion.7
  169.3 1.3 collective-permute-start.1
  170.8 2.5 fusion.11
  175.9 1.3 add_convert_fusion.5
  179.6 1.5 slice-done.5
  181.9 3.0 fusion.44
  184.9 2.9 fusion.48
  188.3 3.6 multiply_convert_fusion.3
  191.9 4.3 fusion.73
  196.2 5.7 %multiply_convert_fusion.2 = (bf16[8,64,2048]{2,1,0:T(8,128)(2,1)}, f32[8,64,2048]{2,1,0:T(8,128)}) fusion(f32[8,64]{1,0:T(8,128)S(1)} %get-tuple-element.60, bf16[8,64,128]{1,2,0:T(8,128)(2,1)S(1)} %fusion.112, bf16[2,8,128,2048]{3,2,1,0:T(8,128)(2,1)} %get-tuple-element.16), kind=kOutput, calls=%fused_computation.36 | convolution fusion | flops 270532608 | bytes 10618880 | tf_op jit(solution)/shard_map/dot_general | solution.py:155
  201.9 6.7 %multiply_convert_fusion.7 = (bf16[512,768]{1,0:T(8,128)(2,1)S(1)}, bf16[512,768]{1,0:T(8,128)(2,1)S(1)}, bf16[512,768]{1,0:T(8,128)(2,1)}) fusion(f32[512,768]{1,0:T(8,128)} %fusion.44, f32[512,768]{1,0:T(8,128)} %fusion.48, bf16[512,2048]{1,0:T(8,128)(2,1)} %bitcast.213, bf16[2,768,2048]{2,1,0:T(8,128)(2,1)} %param.15), kind=kOutput, calls=%fused_computation.101 | convolution fusion | flops 1616510976 | bytes 10747904 | tf_op jit(solution)/shard_map/dot_general | solution.py:151
  211.7 1.3 fusion.80
  213.0 1.3 fusion.82
  217.1 1.5 fusion.84
  218.6 2.3 add_convert_fusion.3
  220.9 2.3 add_convert_fusion.4
  223.5 1.9 copy-done.2
  225.4 1.6 fusion.8
  227.0 2.1 fusion.113
  229.3 2.3 add_convert_fusion.2
  231.5 1.6 add_convert_fusion.13
  233.1 2.3 add_convert_fusion.12
  235.4 2.3 add_convert_fusion.11
  237.7 1.8 multiply_convert_fusion
  239.6 1.8 multiply_convert_fusion.1
  241.4 2.9 fusion.31
  246.6 1.3 constant_dynamic-slice_fusion.1
  247.8 1.3 collective-permute-start.4
  250.1 16.2 %collective-permute-done.3 = bf16[192,2048]{1,0:T(8,128)(2,1)S(1)} collective-permute-done((bf16[192,2048]{1,0:T(8,128)(2,1)S(1)}, bf16[192,2048]{1,0:T(8,128)(2,1)S(1)}, u32[]{:S(2)}, u32[]{:S(2)}) %collective-permute-start.3) | collective-permute-done | bytes 786464 | tf_op jit(solution)/shard_map/ppermute | solution.py:248
  267.4 15.7 %collective-permute-done.4 = bf16[192,2048]{1,0:T(8,128)(2,1)S(1)} collective-permute-done((bf16[192,2048]{1,0:T(8,128)(2,1)S(1)}, bf16[192,2048]{1,0:T(8,128)(2,1)S(1)}, u32[]{:S(2)}, u32[]{:S(2)}) %collective-permute-start.4) | collective-permute-done | bytes 786464 | tf_op jit(solution)/shard_map/ppermute | solution.py:248
  284.3 14.6 %collective-permute-done.5 = bf16[192,2048]{1,0:T(8,128)(2,1)S(1)} collective-permute-done((bf16[192,2048]{1,0:T(8,128)(2,1)S(1)}, bf16[192,2048]{1,0:T(8,128)(2,1)S(1)}, u32[]{:S(2)}, u32[]{:S(2)}) %collective-permute-start.5) | collective-permute-done | bytes 786464 | tf_op jit(solution)/shard_map/ppermute | solution.py:248
  300.1 3.9 fusion.42
  304.0 1.8 fusion.56
  305.9 1.8 add_convert_fusion
  307.7 1.8 add_convert_fusion.1
  309.6 3.4 fusion.28
  318.8 14.7 %collective-permute-done.6 = bf16[192,2048]{1,0:T(8,128)(2,1)} collective-permute-done((bf16[192,2048]{1,0:T(8,128)(2,1)S(1)}, bf16[192,2048]{1,0:T(8,128)(2,1)}, u32[]{:S(2)}, u32[]{:S(2)}) %collective-permute-start.6) | collective-permute-done | bytes 786464 | tf_op jit(solution)/shard_map/ppermute | solution.py:274
  334.1 2.3 bitcast_dynamic-update-slice_fusion.5
  336.4 25.2 %collective-permute-done.7 = bf16[192,2048]{1,0:T(8,128)(2,1)} collective-permute-done((bf16[192,2048]{1,0:T(8,128)(2,1)S(1)}, bf16[192,2048]{1,0:T(8,128)(2,1)}, u32[]{:S(2)}, u32[]{:S(2)}) %collective-permute-start.7) | collective-permute-done | bytes 786464 | tf_op jit(solution)/shard_map/ppermute | solution.py:274
  361.7 2.3 bitcast_dynamic-update-slice_fusion.4
  364.0 20.0 %collective-permute-done.8 = bf16[192,2048]{1,0:T(8,128)(2,1)S(1)} collective-permute-done((bf16[192,2048]{1,0:T(8,128)(2,1)S(1)}, bf16[192,2048]{1,0:T(8,128)(2,1)S(1)}, u32[]{:S(2)}, u32[]{:S(2)}) %collective-permute-start.8) | collective-permute-done | bytes 786464 | tf_op jit(solution)/shard_map/ppermute | solution.py:274
  385.2 15.7 %collective-permute-done.9 = bf16[192,2048]{1,0:T(8,128)(2,1)S(1)} collective-permute-done((bf16[192,2048]{1,0:T(8,128)(2,1)S(1)}, bf16[192,2048]{1,0:T(8,128)(2,1)S(1)}, u32[]{:S(2)}, u32[]{:S(2)}) %collective-permute-start.9) | collective-permute-done | bytes 786464 | tf_op jit(solution)/shard_map/ppermute | solution.py:274
  402.0 15.7 %collective-permute-done.10 = bf16[192,2048]{1,0:T(8,128)(2,1)S(1)} collective-permute-done((bf16[192,2048]{1,0:T(8,128)(2,1)}, bf16[192,2048]{1,0:T(8,128)(2,1)S(1)}, u32[]{:S(2)}, u32[]{:S(2)}) %collective-permute-start.10) | collective-permute-done | bytes 786464 | tf_op jit(solution)/shard_map/ppermute | solution.py:274
  418.9 13.7 %collective-permute-done.11 = bf16[192,2048]{1,0:T(8,128)(2,1)S(1)} collective-permute-done((bf16[192,2048]{1,0:T(8,128)(2,1)}, bf16[192,2048]{1,0:T(8,128)(2,1)S(1)}, u32[]{:S(2)}, u32[]{:S(2)}) %collective-permute-start.11) | collective-permute-done | bytes 786464 | tf_op jit(solution)/shard_map/ppermute | solution.py:274
  433.9 9.4 %copy.19 = bf16[192,2,3,2048]{3,1,2,0:T(2,128)(2,1)} copy(bf16[192,2,3,2048]{3,0,2,1:T(8,128)(2,1)} %bitcast.42) | data formatting | bytes 9437184
  (200 shorter events, 43.0 us)
Async XLA Ops:
  7.2 436.1 %reduce-scatter.3.cloned.1.call-start = ((), (), s32[]{:S(2)}) async-start(), calls=%async_computation.2 | async-start | bytes 4718592 | tf_op jit(solution)/shard_map/reduce_scatter | solution.py:267
  105.6 7.3 %copy-start = (bf16[2,8,128,2048]{3,2,1,0:T(8,128)(2,1)S(1)}, bf16[2,8,128,2048]{3,2,1,0:T(8,128)(2,1)}, u32[]{:S(2)}) copy-start(bf16[2,8,128,2048]{3,2,1,0:T(8,128)(2,1)} %get-tuple-element.15) | copy-start | bytes 25165828
  105.6 9.3 %copy-start.10 = (bf16[2,2048,768]{2,1,0:T(8,128)(2,1)S(1)}, bf16[2,2048,768]{2,1,0:T(8,128)(2,1)}, u32[]{:S(2)}) copy-start(bf16[2,2048,768]{2,1,0:T(8,128)(2,1)} %param.13) | copy-start | bytes 18874372
  105.6 12.3 %slice-start.6 = ((s8[6291456]{0:T(1024)(128)(4,1)}), s8[4194304]{0:T(1024)(128)(4,1)S(1)}, s32[]{:S(2)}) async-start(s8[6291456]{0:T(1024)(128)(4,1)} %bitcast.198), calls=%async_computation.10 | async-start | bytes 8388608
  112.9 5.0 %slice-start.7 = ((s8[6291456]{0:T(1024)(128)(4,1)}), s8[2097152]{0:T(1024)(128)(4,1)S(1)}, s32[]{:S(2)}) async-start(s8[6291456]{0:T(1024)(128)(4,1)} %bitcast.198), calls=%async_computation.11 | async-start | bytes 4194304
  114.9 7.4 %slice-start = ((s8[8388608]{0:T(1024)(128)(4,1)}), s8[4194304]{0:T(1024)(128)(4,1)S(1)}, s32[]{:S(2)}) async-start(s8[8388608]{0:T(1024)(128)(4,1)} %bitcast.176), calls=%async_computation.4 | async-start | bytes 8388608
  118.0 4.4 slice-start.1
  128.4 12.8 %slice-start.10 = ((s8[6291456]{0:T(1024)(128)(4,1)}), s8[4194304]{0:T(1024)(128)(4,1)S(1)}, s32[]{:S(2)}) async-start(s8[6291456]{0:T(1024)(128)(4,1)} %bitcast.202), calls=%async_computation.14 | async-start | bytes 8388608
  134.9 6.3 %slice-start.11 = ((s8[6291456]{0:T(1024)(128)(4,1)}), s8[2097152]{0:T(1024)(128)(4,1)S(1)}, s32[]{:S(2)}) async-start(s8[6291456]{0:T(1024)(128)(4,1)} %bitcast.202), calls=%async_computation.15 | async-start | bytes 4194304
  141.2 3.1 copy-start.46
  141.3 3.2 copy-start.47
  147.8 2.7 copy-start.35
  147.8 2.7 copy-start.4
  147.8 3.9 copy-start.19
  150.5 2.5 copy-start.21
  153.0 2.8 copy-start.24
  158.0 6.4 %copy-start.37 = (bf16[512,768]{1,0:T(8,128)(2,1)S(1)}, bf16[512,768]{1,0:T(8,128)(2,1)}, u32[]{:S(2)}) copy-start(bf16[512,768]{1,0:T(8,128)(2,1)} %get-tuple-element.22) | copy-start | bytes 2359300
  164.3 67.2 %collective-permute-start = (bf16[192,2048]{1,0:T(8,128)(2,1)}, bf16[192,2048]{1,0:T(8,128)(2,1)}, u32[]{:S(2)}, u32[]{:S(2)}) collective-permute-start(bf16[192,2048]{1,0:T(8,128)(2,1)} %constant_dynamic-slice_fusion.5), channel_id=1, source_target_pairs={{0,1},{1,0},{2,3},{3,2},{4,5},{5,4},{6,7},{7,6},{8,9},{9,8},{10,11... | collective-permute-start | bytes 2359304 | tf_op jit(solution)/shard_map/ppermute | solution.py:248
  169.3 63.8 %collective-permute-start.1 = (bf16[192,2048]{1,0:T(8,128)(2,1)}, bf16[192,2048]{1,0:T(8,128)(2,1)}, u32[]{:S(2)}, u32[]{:S(2)}) collective-permute-start(bf16[192,2048]{1,0:T(8,128)(2,1)} %constant_dynamic-slice_fusion.4), channel_id=1, source_target_pairs={{0,1},{1,0},{2,3},{3,2},{4,5},{5,4},{6,7},{7,6},{8,9},{9,8},{10,11... | collective-permute-start | bytes 2359304 | tf_op jit(solution)/shard_map/ppermute | solution.py:248
  170.8 2.6 copy-start.39
  173.4 2.5 copy-start.31
  175.5 4.0 slice-start.4
  175.5 6.4 %slice-start.16 = ((s8[6291456]{0:T(1024)(128)(4,1)}), s8[4194304]{0:T(1024)(128)(4,1)S(1)}, s32[]{:S(2)}) async-start(s8[6291456]{0:T(1024)(128)(4,1)} %bitcast.208), calls=%async_computation.20 | async-start | bytes 8388608
  175.8 5.3 %slice-start.5 = ((s8[8388608]{0:T(1024)(128)(4,1)}), s8[4194304]{0:T(1024)(128)(4,1)S(1)}, s32[]{:S(2)}) async-start(s8[8388608]{0:T(1024)(128)(4,1)} %bitcast.180), calls=%async_computation.9 | async-start | bytes 8388608
  175.8 6.1 %slice-start.17 = ((s8[6291456]{0:T(1024)(128)(4,1)}), s8[2097152]{0:T(1024)(128)(4,1)S(1)}, s32[]{:S(2)}) async-start(s8[6291456]{0:T(1024)(128)(4,1)} %bitcast.208), calls=%async_computation.21 | async-start | bytes 4194304
  175.9 9.1 %slice-start.12 = ((s8[6291456]{0:T(1024)(128)(4,1)}), s8[4194304]{0:T(1024)(128)(4,1)S(1)}, s32[]{:S(2)}) async-start(s8[6291456]{0:T(1024)(128)(4,1)} %bitcast.204), calls=%async_computation.16 | async-start | bytes 8388608
  177.1 4.8 %copy-start.27 = (bf16[384,2048]{1,0:T(8,128)(2,1)}, bf16[384,2048]{1,0:T(8,128)(2,1)S(1)}, u32[]{:S(2)}) copy-start(bf16[384,2048]{1,0:T(8,128)(2,1)S(1)} %add_convert_fusion.5) | copy-start | bytes 4718596
  178.1 57.3 %collective-permute-start.2 = (bf16[192,2048]{1,0:T(8,128)(2,1)}, bf16[192,2048]{1,0:T(8,128)(2,1)}, u32[]{:S(2)}, u32[]{:S(2)}) collective-permute-start(bf16[192,2048]{1,0:T(8,128)(2,1)} %constant_dynamic-slice_fusion.3), channel_id=1, source_target_pairs={{0,1},{1,0},{2,3},{3,2},{4,5},{5,4},{6,7},{7,6},{8,9},{9,8},{10,11... | collective-permute-start | bytes 2359304 | tf_op jit(solution)/shard_map/ppermute | solution.py:248
  181.1 3.8 slice-start.13
  181.9 6.3 %slice-start.2 = ((s8[8388608]{0:T(1024)(128)(4,1)}), s8[4194304]{0:T(1024)(128)(4,1)S(1)}, s32[]{:S(2)}) async-start(s8[8388608]{0:T(1024)(128)(4,1)} %bitcast.178), calls=%async_computation.6 | async-start | bytes 8388608
  184.9 3.3 slice-start.3
  208.6 5.7 %copy-start.41 = (bf16[512,768]{1,0:T(8,128)(2,1)}, bf16[512,768]{1,0:T(8,128)(2,1)S(1)}, u32[]{:S(2)}) copy-start(bf16[512,768]{1,0:T(8,128)(2,1)S(1)} %get-tuple-element.24) | copy-start | bytes 2359300
  208.6 3.1 copy-start.17
  209.7 3.3 copy-start.18
  214.3 6.6 %copy-start.32 = (f32[512,384]{1,0:T(8,128)}, f32[512,384]{1,0:T(8,128)S(1)}, u32[]{:S(2)}) copy-start(f32[512,384]{1,0:T(8,128)S(1)} %fusion.82) | copy-start | bytes 2359300
  214.3 2.8 copy-start.22
  220.9 2.4 copy-start.1
  227.0 10.7 %slice-start.8 = ((s8[6291456]{0:T(1024)(128)(4,1)}), s8[4194304]{0:T(1024)(128)(4,1)S(1)}, s32[]{:S(2)}) async-start(s8[6291456]{0:T(1024)(128)(4,1)} %bitcast.200), calls=%async_computation.12 | async-start | bytes 8388608
  229.2 2.3 copy-start.8
  229.2 3.9 copy-start.26
  229.2 8.5 %slice-start.9 = ((s8[6291456]{0:T(1024)(128)(4,1)}), s8[2097152]{0:T(1024)(128)(4,1)S(1)}, s32[]{:S(2)}) async-start(s8[6291456]{0:T(1024)(128)(4,1)} %bitcast.200), calls=%async_computation.13 | async-start | bytes 4194304
  231.5 3.9 copy-start.28
  231.5 6.2 %copy-start.45 = (bf16[512,768]{1,0:T(8,128)(2,1)S(1)}, bf16[512,768]{1,0:T(8,128)(2,1)}, u32[]{:S(2)}) copy-start(bf16[512,768]{1,0:T(8,128)(2,1)} %get-tuple-element.20) | copy-start | bytes 2359300
  244.3 198.9 %reduce-scatter.5.cloned.1.call-start = ((), (), s32[]{:S(2)}) async-start(), calls=%async_computation.3 | async-start | bytes 4718592 | tf_op jit(solution)/shard_map/reduce_scatter | solution.py:267
  245.7 3.4 copy-start.30
  245.8 37.3 %copy-start.29 = (bf16[384,2048]{1,0:T(8,128)(2,1)S(1)}, bf16[384,2048]{1,0:T(8,128)(2,1)}, u32[]{:S(2)}) copy-start(bf16[384,2048]{1,0:T(8,128)(2,1)} %add_convert_fusion.3) | copy-start | bytes 4718596
  245.8 20.5 %collective-permute-start.3 = (bf16[192,2048]{1,0:T(8,128)(2,1)S(1)}, bf16[192,2048]{1,0:T(8,128)(2,1)S(1)}, u32[]{:S(2)}, u32[]{:S(2)}) collective-permute-start(bf16[192,2048]{1,0:T(8,128)(2,1)S(1)} %constant_dynamic-slice_fusion.2), channel_id=1, source_target_pairs={{0,1},{1,0},{2,3},{3,2},{4,5},{5,4},{6,7},{7,6},{8,9},{9,8},{10,11... | collective-permute-start | bytes 2359304 | tf_op jit(solution)/shard_map/ppermute | solution.py:248
  247.8 35.3 %collective-permute-start.4 = (bf16[192,2048]{1,0:T(8,128)(2,1)S(1)}, bf16[192,2048]{1,0:T(8,128)(2,1)S(1)}, u32[]{:S(2)}, u32[]{:S(2)}) collective-permute-start(bf16[192,2048]{1,0:T(8,128)(2,1)S(1)} %constant_dynamic-slice_fusion.1), channel_id=1, source_target_pairs={{0,1},{1,0},{2,3},{3,2},{4,5},{5,4},{6,7},{7,6},{8,9},{9,8},{10,11... | collective-permute-start | bytes 2359304 | tf_op jit(solution)/shard_map/ppermute | solution.py:248
  249.2 50.9 %copy-start.44 = (bf16[512,768]{1,0:T(8,128)(2,1)S(1)}, bf16[512,768]{1,0:T(8,128)(2,1)}, u32[]{:S(2)}) copy-start(bf16[512,768]{1,0:T(8,128)(2,1)} %copy-done.43) | copy-start | bytes 2359300
  249.2 49.7 %collective-permute-start.5 = (bf16[192,2048]{1,0:T(8,128)(2,1)S(1)}, bf16[192,2048]{1,0:T(8,128)(2,1)S(1)}, u32[]{:S(2)}, u32[]{:S(2)}) collective-permute-start(bf16[192,2048]{1,0:T(8,128)(2,1)S(1)} %constant_dynamic-slice_fusion), channel_id=1, source_target_pairs={{0,1},{1,0},{2,3},{3,2},{4,5},{5,4},{6,7},{7,6},{8,9},{9,8},{10,11... | collective-permute-start | bytes 2359304 | tf_op jit(solution)/shard_map/ppermute | solution.py:248
  283.1 20.8 %slice-start.14 = ((s8[6291456]{0:T(1024)(128)(4,1)}), s8[4194304]{0:T(1024)(128)(4,1)S(1)}, s32[]{:S(2)}) async-start(s8[6291456]{0:T(1024)(128)(4,1)} %bitcast.206), calls=%async_computation.18 | async-start | bytes 8388608
  300.1 3.9 slice-start.15
  300.1 3.9 copy-start.38
  304.0 3.7 slice-start.18
  312.9 2.8 copy-start.12
  313.0 3.9 copy-start.13
  313.0 20.6 %collective-permute-start.6 = (bf16[192,2048]{1,0:T(8,128)(2,1)S(1)}, bf16[192,2048]{1,0:T(8,128)(2,1)}, u32[]{:S(2)}, u32[]{:S(2)}) collective-permute-start(bf16[192,2048]{1,0:T(8,128)(2,1)S(1)} %add_convert_fusion.13), channel_id=1, source_target_pairs={{0,16},{4,20},{8,24},{12,28},{16,0},{20,4},{24,8},{28,12},{1,17},{... | collective-permute-start | bytes 2359304 | tf_op jit(solution)/shard_map/ppermute | solution.py:274
  314.1 47.6 %collective-permute-start.7 = (bf16[192,2048]{1,0:T(8,128)(2,1)S(1)}, bf16[192,2048]{1,0:T(8,128)(2,1)}, u32[]{:S(2)}, u32[]{:S(2)}) collective-permute-start(bf16[192,2048]{1,0:T(8,128)(2,1)S(1)} %copy-done.11), channel_id=1, source_target_pairs={{0,16},{4,20},{8,24},{12,28},{16,0},{20,4},{24,8},{28,12},{1,17},{... | collective-permute-start | bytes 2359304 | tf_op jit(solution)/shard_map/ppermute | solution.py:274
  315.7 68.3 %collective-permute-start.8 = (bf16[192,2048]{1,0:T(8,128)(2,1)S(1)}, bf16[192,2048]{1,0:T(8,128)(2,1)S(1)}, u32[]{:S(2)}, u32[]{:S(2)}) collective-permute-start(bf16[192,2048]{1,0:T(8,128)(2,1)S(1)} %copy-done.12), channel_id=1, source_target_pairs={{0,16},{4,20},{8,24},{12,28},{16,0},{20,4},{24,8},{28,12},{1,17},{... | collective-permute-start | bytes 2359304 | tf_op jit(solution)/shard_map/ppermute | solution.py:274
  316.8 84.1 %collective-permute-start.9 = (bf16[192,2048]{1,0:T(8,128)(2,1)S(1)}, bf16[192,2048]{1,0:T(8,128)(2,1)S(1)}, u32[]{:S(2)}, u32[]{:S(2)}) collective-permute-start(bf16[192,2048]{1,0:T(8,128)(2,1)S(1)} %copy-done.13), channel_id=1, source_target_pairs={{0,16},{4,20},{8,24},{12,28},{16,0},{20,4},{24,8},{28,12},{1,17},{... | collective-permute-start | bytes 2359304 | tf_op jit(solution)/shard_map/ppermute | solution.py:274
  317.8 99.9 %collective-permute-start.10 = (bf16[192,2048]{1,0:T(8,128)(2,1)}, bf16[192,2048]{1,0:T(8,128)(2,1)S(1)}, u32[]{:S(2)}, u32[]{:S(2)}) collective-permute-start(bf16[192,2048]{1,0:T(8,128)(2,1)} %add_convert_fusion.9), channel_id=1, source_target_pairs={{0,16},{4,20},{8,24},{12,28},{16,0},{20,4},{24,8},{28,12},{1,17},{... | collective-permute-start | bytes 2359304 | tf_op jit(solution)/shard_map/ppermute | solution.py:274
  333.6 99.1 %collective-permute-start.11 = (bf16[192,2048]{1,0:T(8,128)(2,1)}, bf16[192,2048]{1,0:T(8,128)(2,1)S(1)}, u32[]{:S(2)}, u32[]{:S(2)}) collective-permute-start(bf16[192,2048]{1,0:T(8,128)(2,1)} %add_convert_fusion.8), channel_id=1, source_target_pairs={{0,16},{4,20},{8,24},{12,28},{16,0},{20,4},{24,8},{28,12},{1,17},{... | collective-permute-start | bytes 2359304 | tf_op jit(solution)/shard_map/ppermute | solution.py:274
  336.4 81.3 %copy-start.14 = (bf16[192,2048]{1,0:T(8,128)(2,1)S(1)}, bf16[192,2048]{1,0:T(8,128)(2,1)}, u32[]{:S(2)}) copy-start(bf16[192,2048]{1,0:T(8,128)(2,1)} %add_convert_fusion.9) | copy-start | bytes 2359300
  364.0 68.7 %copy-start.15 = (bf16[192,2048]{1,0:T(8,128)(2,1)S(1)}, bf16[192,2048]{1,0:T(8,128)(2,1)}, u32[]{:S(2)}) copy-start(bf16[192,2048]{1,0:T(8,128)(2,1)} %add_convert_fusion.8) | copy-start | bytes 2359300
  (18 other events, 31.9 us)
Sparse Core Ops, SparseCore 0:
  244.4 51.2 reduce-scatter.2
  313.1 68.2 reduce-scatter.4
